TPU v7x, 32 devices: a whole 2x2x4 slice. The times are simulated.
32 devices in a mesh: groups: 2 (over y), atoms: 8 (over z, x), samples: 2 (over core).
Axes of the slice: x: 2, y: 2, z: 4, core: 2. Of those that a mesh axis runs over, the one named last changes fastest.
Arguments:
- act: bfloat16 [16, 10240, 128], P('samples', ('groups', 'atoms')), parts along dimension 1, may hold values from -6 to 6
- grad_out: bfloat16 [16, 10240, 128], P('samples', ('groups', 'atoms')), parts along dimension 1, may hold values from -6 to 6
- pair: bfloat16 [320, 32, 16, 128], P(('groups', 'atoms')), parts along dimension 0, may hold values from -500 to 500
- w_query: bfloat16 [128, 128], replicated, may hold values from -0.5 to 0.5
- w_key: bfloat16 [128, 128], replicated, may hold values from -0.5 to 0.5
- w_value: bfloat16 [128, 128], replicated, may hold values from -0.5 to 0.5
- w_gate: bfloat16 [128, 128], replicated, may hold values from -0.5 to 0.5
- w_out: bfloat16 [128, 128], replicated, may hold values from -0.5 to 0.5
- w_pair: bfloat16 [16, 4], replicated, may hold values from -1.5 to 1.5
- w_token: float32 [4], replicated, may hold values from -2 to 2
- offsets: int32 [320], P(('groups', 'atoms')), parts along dimension 0, may hold values from -128 to 32, as said below
- atom_token: int32 [10240], P(('groups', 'atoms')), parts along dimension 0, may hold values from 0 to 639, never falling along the last dimension, each value on 1 to 24 neighbouring positions
- padding: int32 [16], P(('groups', 'atoms')), parts along dimension 0, may hold values from 0 to 64, as said below
Outputs:
- grad_act: bfloat16 [16, 10240, 128], P('samples', ('groups', 'atoms')), parts along dimension 1
- grad_pair: bfloat16 [320, 32, 16, 128], P(('groups', 'atoms'), 'samples'), parts along dimension 0
- grad_weights: float32 [10, 128, 128], P('groups'), parts along dimension 0
- grad_pair_weight: float32 [32, 4], P('groups'), parts along dimension 0
- grad_token_weight: float32 [8], P('groups'), parts along dimension 0
There are 2 independent parts, one for each index of `groups`. A program takes and returns all parts, laid end to end along the dimension named above; an argument that names none is the same for every part. Nothing has to cross between parts.
Inputs may be any that keep to these rules, and one draw needn't show every extreme that they name: Window w reads the 128 atoms that begin at 32 * w + offsets[w], moved into the complex. padding[r] atoms at the end of atom range r are padding. `atom_token`: the atoms of one token are contiguous, at most 24 of them.
All inputs are finite; a program needn't handle non-finite values.
Results may differ from a plain program's by a relative error of at most 0.025.
Values may be sent and summed in bfloat16 or wider, within the bound.
A program may use at most 128 MiB of HBM per device.

v0:
```python
import math

import jax
import jax.numpy as jnp
from jax import lax
from jax.sharding import PartitionSpec as P

MASKED = -1000000000.0


def with_halo(value, sides, width):
    for axis, dim in sides:
        count, length = (lax.axis_size(axis), value.shape[dim])
        up = [(i, (i + 1) % count) for i in range(count - 1)]
        down = [(j, i) for i, j in up]
        last = lax.slice_in_dim(value, length - width, length, axis=dim)
        initial = lax.slice_in_dim(value, 0, width, axis=dim)
        before = lax.ppermute(last, axis, up)
        after = lax.ppermute(initial, axis, down)
        value = jnp.concatenate([before, value, after], axis=dim)
    return value


def passed_along(value, axis, steps):
    count = lax.axis_size(axis)
    initial, last = (max(0, -steps), min(count, count - steps))
    return lax.ppermute(value, axis, [(source, source + steps) for source in range(initial, last)])


def attend(query, keys, values, gate_logit, grad_y, pair_bias, key_live):
    windows = keys.shape[0]
    head_count = pair_bias.shape[1]
    channels = query.shape[-1]
    head_dim = channels // head_count
    score_scale = 1.0 / math.sqrt(head_dim)
    query_heads = query.reshape(windows, -1, head_count, head_dim)
    key_heads = keys.reshape(windows, -1, head_count, head_dim)
    value_heads = values.reshape(windows, -1, head_count, head_dim)
    scores = (
        jnp.einsum("wihd,wjhd->whij", query_heads, key_heads, preferred_element_type=jnp.float32)
        * score_scale
        + pair_bias
    )
    scores = jnp.where(key_live[:, None, None, :], scores, MASKED)
    row_max = jnp.max(scores, axis=-1, keepdims=True)
    exponent = jnp.exp(scores - row_max)
    attn_probs = exponent / jnp.sum(exponent, axis=-1, keepdims=True)
    probs_b = attn_probs.astype(jnp.bfloat16)
    attended = jnp.einsum(
        "whij,wjhd->wihd", probs_b, value_heads, preferred_element_type=jnp.float32
    ).reshape(query.shape)
    gate_value = jax.nn.sigmoid(gate_logit)
    gated = (gate_value * attended).astype(jnp.bfloat16)
    d_attended = (grad_y * gate_value).astype(jnp.bfloat16)
    d_gate = (grad_y * attended * gate_value * (1.0 - gate_value)).astype(jnp.bfloat16)
    attended_heads = d_attended.reshape(windows, -1, head_count, head_dim)
    d_probs = jnp.einsum(
        "wihd,wjhd->whij", attended_heads, value_heads, preferred_element_type=jnp.float32
    )
    d_scores = attn_probs * (d_probs - jnp.sum(attn_probs * d_probs, axis=-1, keepdims=True))
    ds_b = d_scores.astype(jnp.bfloat16)
    d_query = (
        (
            jnp.einsum("whij,wjhd->wihd", ds_b, key_heads, preferred_element_type=jnp.float32)
            * score_scale
        )
        .astype(jnp.bfloat16)
        .reshape(query.shape)
    )
    d_keys = (
        jnp.einsum("whij,wihd->wjhd", ds_b, query_heads, preferred_element_type=jnp.float32)
        * score_scale
    )
    d_values = jnp.einsum(
        "whij,wihd->wjhd", probs_b, attended_heads, preferred_element_type=jnp.float32
    )
    return (gated, d_query, d_gate, d_keys, d_values, d_scores)


def per_device(
    act,
    grad_out,
    pair,
    w_query,
    w_key,
    w_value,
    w_gate,
    w_out,
    w_pair,
    w_token,
    offsets,
    atom_token,
    padding,
):
    sample_count, atom_count, channels = act.shape
    windows = offsets.shape[0]
    win_rows = atom_count // windows
    key_span = pair.shape[-1]
    ranges = lax.axis_size("atoms")
    anchor = lax.axis_index("atoms") * atom_count
    position = jnp.arange(atom_count, dtype=jnp.int32)
    is_live = position < atom_count - padding[0]
    atom_codes = jnp.where(is_live, atom_token + 1, 0)
    wide_codes = with_halo(atom_codes, (("atoms", 0),), key_span)
    starts = jnp.clip(
        anchor + win_rows * jnp.arange(windows, dtype=jnp.int32) + offsets,
        0,
        ranges * atom_count - key_span,
    )
    key_rows = starts[:, None] - anchor + key_span + jnp.arange(key_span, dtype=jnp.int32)[None, :]
    key_codes = wide_codes[key_rows]
    key_live = key_codes > 0
    same_token = key_codes[:, None, :] == (atom_token + 1).reshape(windows, win_rows)[:, :, None]
    pair_bias = jnp.einsum(
        "wicj,ch->whij", pair, w_pair, preferred_element_type=jnp.float32
    ) + w_token[None, :, None, None] * same_token[:, None, :, :].astype(jnp.float32)
    projection = jnp.concatenate([w_query, w_key, w_value, w_gate], axis=1)
    flat_act = act.reshape(sample_count * atom_count, channels)
    mixed = jnp.dot(flat_act, projection, preferred_element_type=jnp.float32).reshape(
        sample_count, atom_count, 4 * channels
    )
    query = mixed[..., :channels].astype(jnp.bfloat16)
    key_value = mixed[..., channels : 3 * channels].astype(jnp.bfloat16)
    gate_logit = mixed[..., 3 * channels :]
    wide_kv = with_halo(key_value, (("atoms", 1),), key_span)
    flat_grad = grad_out.reshape(sample_count * atom_count, channels)
    grad_y = jnp.dot(flat_grad, w_out.T, preferred_element_type=jnp.float32).reshape(
        sample_count, atom_count, channels
    )

    def one_sample(bias_sum, inputs):
        sample_query, sample_kv, sample_gate, sample_grad_y = inputs
        windowed = sample_kv[key_rows]
        gated, d_query, d_gate, d_keys, d_values, d_scores = attend(
            sample_query,
            windowed[..., :channels],
            windowed[..., channels:],
            sample_gate,
            sample_grad_y,
            pair_bias,
            key_live,
        )
        d_windowed = jnp.concatenate(
            [
                d_keys.reshape(windows, key_span, channels),
                d_values.reshape(windows, key_span, channels),
            ],
            axis=-1,
        )
        d_wide = jnp.zeros(sample_kv.shape, jnp.float32).at[key_rows].add(d_windowed)
        return (bias_sum + d_scores, (gated, d_query, d_gate, d_wide))

    bias_local, (gated, d_query, d_gate, d_wide) = lax.scan(
        one_sample, jnp.zeros(pair_bias.shape, jnp.float32), (query, wide_kv, gate_logit, grad_y)
    )
    inner_grad = d_wide[:, key_span : key_span + atom_count]
    from_upper = passed_along(d_wide[:, :key_span].astype(jnp.bfloat16), "atoms", -1).astype(
        jnp.float32
    )
    from_lower = passed_along(
        d_wide[:, key_span + atom_count :].astype(jnp.bfloat16), "atoms", 1
    ).astype(jnp.float32)
    kv_grad = (
        inner_grad.at[:, :key_span].add(from_lower).at[:, atom_count - key_span :].add(from_upper)
    )
    kv_rounded = kv_grad.astype(jnp.bfloat16)
    stacked = jnp.concatenate([d_query, kv_rounded, d_gate], axis=-1).reshape(
        sample_count * atom_count, 4 * channels
    )
    grad_act = (
        jnp.dot(stacked, projection.T, preferred_element_type=jnp.float32)
        .astype(jnp.bfloat16)
        .reshape(sample_count, atom_count, channels)
    )
    weight_part = jnp.dot(flat_act.T, stacked, preferred_element_type=jnp.float32)
    out_part = jnp.dot(gated.reshape(-1, channels).T, flat_grad, preferred_element_type=jnp.float32)
    pair_weight_part = jnp.einsum(
        "wicj,whij->ch", pair, bias_local, preferred_element_type=jnp.float32
    )
    token_part = jnp.sum(jnp.where(same_token[:, None, :, :], bias_local, 0.0), axis=(0, 2, 3))
    weight_sum, out_sum, grad_pair_weight, grad_token_weight = lax.psum(
        (weight_part, out_part, pair_weight_part, token_part), ("atoms", "samples")
    )
    grad_weights = jnp.concatenate(
        [weight_sum.reshape(channels, 4, channels).transpose(1, 0, 2), out_sum[None]], axis=0
    )
    sample_ways = lax.axis_size("samples")
    share_rows = win_rows // sample_ways
    bias_total = lax.psum(bias_local.astype(jnp.bfloat16), "samples").astype(jnp.float32)
    my_share = lax.dynamic_slice_in_dim(
        bias_total, lax.axis_index("samples") * share_rows, share_rows, 2
    )
    grad_pair = jnp.einsum(
        "whij,ch->wicj", my_share, w_pair.astype(jnp.float32), precision=lax.Precision.HIGHEST
    ).astype(jnp.bfloat16)
    return (grad_act, grad_pair, grad_weights, grad_pair_weight, grad_token_weight)


def solution(mesh):
    in_specs = (
        P("samples", ("groups", "atoms"), None),
        P("samples", ("groups", "atoms"), None),
        P(("groups", "atoms"), None, None, None),
        P(),
        P(),
        P(),
        P(),
        P(),
        P(),
        P(),
        P(("groups", "atoms")),
        P(("groups", "atoms")),
        P(("groups", "atoms")),
    )
    out_specs = (
        P("samples", ("groups", "atoms"), None),
        P(("groups", "atoms"), "samples", None, None),
        P("groups", None, None),
        P("groups", None),
        P("groups"),
    )
    return jax.shard_map(
        per_device, mesh=mesh, in_specs=in_specs, out_specs=out_specs, check_vma=False
    )
```

profile of v0, /device:TPU:8, one launch (start us, length us, event | category | flops | bytes accessed | tf_op | source)
XLA Modules:
  0.0 949.7 jit_solution(12060509717389246733)
XLA Ops:
  11.1 6.7 convolution_bitcast_fusion.1
  17.8 11.4 %copy.63 = f32[5120,512]{1,0:T(8,128)} copy(f32[5120,512]{0,1:T(8,128)} %convolution_bitcast_fusion.1) | data formatting | bytes 20971520 | tf_op jit(solution)/shard_map/reshape | solution.py:119
  29.2 4.7 convert.8
  35.1 3.4 collective-permute-start.2
  38.4 3.3 collective-permute-start.3
  45.0 4.2 collective-permute-start.1
  50.6 3.4 slice.115
  57.5 3.7 collective-permute-done
  63.1 9.4 gather_fusion.1
  78.5 686.5 %while.21 = (s32[]{:T(128)}, f32[20,4,32,128]{3,2,1,0:T(8,128)}, bf16[8,640,128]{2,1,0:T(8,128)(2,1)}, bf16[8,640,128]{1,2,0:T(8,128)(2,1)}, bf16[8,640,128]{1,2...) while((s32[]{:T(128)}, f32[20,4,32,128]{3,2,1,0:T(8,128)}, ...), condition=%wide.region_5.6_spmd.clone, body=%wide.region_0.5_spmd.clone.sunk | while | flops 135430016 | bytes 73126840 | solution.py:153
  79.6 8.1 gather_fusion
  99.7 7.5 convolution_bitcast_fusion.5
  116.8 7.5 fusion.113
  133.7 3.3 copy.101
  137.1 15.7 %scatter_custom_fusion.6 = f32[896,256]{1,0:T(8,128)} fusion(s32[2560]{0:T(1024)S(1)} %fusion.106, f32[2560,256]{1,0:T(8,128)} %bitcast.143, f32[]{:T(128)} %constant.105.clone.5..sunk), kind=kCustom, calls=%fused_computation.21.clone.1 | custom fusion | flops 655360 | bytes 918016 | tf_op jit(solution)/shard_map/while/body/eval_jaxpr/scatter-add | solution.py:150
  165.1 8.1 gather_fusion
  185.2 7.5 convolution_bitcast_fusion.5
  202.3 7.5 fusion.113
  213.1 3.4 fusion.110
  219.6 3.3 copy.101
  222.9 15.7 %scatter_custom_fusion.6 = f32[896,256]{1,0:T(8,128)} fusion(s32[2560]{0:T(1024)S(1)} %fusion.106, f32[2560,256]{1,0:T(8,128)} %bitcast.143, f32[]{:T(128)} %constant.105.clone.5..sunk), kind=kCustom, calls=%fused_computation.21.clone.1 | custom fusion | flops 655360 | bytes 918016 | tf_op jit(solution)/shard_map/while/body/eval_jaxpr/scatter-add | solution.py:150
  251.0 8.1 gather_fusion
  271.1 7.5 convolution_bitcast_fusion.5
  288.2 7.5 fusion.113
  295.7 3.3 multiply_reduce_fusion.2
  299.0 3.4 fusion.110
  308.8 15.7 %scatter_custom_fusion.6 = f32[896,256]{1,0:T(8,128)} fusion(s32[2560]{0:T(1024)S(1)} %fusion.106, f32[2560,256]{1,0:T(8,128)} %bitcast.143, f32[]{:T(128)} %constant.105.clone.5..sunk), kind=kCustom, calls=%fused_computation.21.clone.1 | custom fusion | flops 655360 | bytes 918016 | tf_op jit(solution)/shard_map/while/body/eval_jaxpr/scatter-add | solution.py:150
  336.8 8.1 gather_fusion
  356.9 7.5 convolution_bitcast_fusion.5
  374.0 7.5 fusion.113
  381.5 3.3 multiply_reduce_fusion.2
  384.9 3.4 fusion.110
  394.6 15.7 %scatter_custom_fusion.6 = f32[896,256]{1,0:T(8,128)} fusion(s32[2560]{0:T(1024)S(1)} %fusion.106, f32[2560,256]{1,0:T(8,128)} %bitcast.143, f32[]{:T(128)} %constant.105.clone.5..sunk), kind=kCustom, calls=%fused_computation.21.clone.1 | custom fusion | flops 655360 | bytes 918016 | tf_op jit(solution)/shard_map/while/body/eval_jaxpr/scatter-add | solution.py:150
  422.7 8.1 gather_fusion
  442.8 7.5 convolution_bitcast_fusion.5
  459.9 7.5 fusion.113
  470.7 3.4 fusion.110
  477.1 3.3 copy.101
  480.5 15.7 %scatter_custom_fusion.6 = f32[896,256]{1,0:T(8,128)} fusion(s32[2560]{0:T(1024)S(1)} %fusion.106, f32[2560,256]{1,0:T(8,128)} %bitcast.143, f32[]{:T(128)} %constant.105.clone.5..sunk), kind=kCustom, calls=%fused_computation.21.clone.1 | custom fusion | flops 655360 | bytes 918016 | tf_op jit(solution)/shard_map/while/body/eval_jaxpr/scatter-add | solution.py:150
  508.5 8.1 gather_fusion
  528.6 7.5 convolution_bitcast_fusion.5
  545.7 7.5 fusion.113
  553.2 3.3 multiply_reduce_fusion.2
  556.6 3.4 fusion.110
  563.0 3.3 copy.101
  566.3 15.7 %scatter_custom_fusion.6 = f32[896,256]{1,0:T(8,128)} fusion(s32[2560]{0:T(1024)S(1)} %fusion.106, f32[2560,256]{1,0:T(8,128)} %bitcast.143, f32[]{:T(128)} %constant.105.clone.5..sunk), kind=kCustom, calls=%fused_computation.21.clone.1 | custom fusion | flops 655360 | bytes 918016 | tf_op jit(solution)/shard_map/while/body/eval_jaxpr/scatter-add | solution.py:150
  594.4 8.1 gather_fusion
  614.5 7.5 convolution_bitcast_fusion.5
  631.6 7.5 fusion.113
  639.1 3.3 multiply_reduce_fusion.2
  642.4 3.4 fusion.110
  652.2 15.7 %scatter_custom_fusion.6 = f32[896,256]{1,0:T(8,128)} fusion(s32[2560]{0:T(1024)S(1)} %fusion.106, f32[2560,256]{1,0:T(8,128)} %bitcast.143, f32[]{:T(128)} %constant.105.clone.5..sunk), kind=kCustom, calls=%fused_computation.21.clone.1 | custom fusion | flops 655360 | bytes 918016 | tf_op jit(solution)/shard_map/while/body/eval_jaxpr/scatter-add | solution.py:150
  680.3 8.1 gather_fusion
  700.4 7.5 convolution_bitcast_fusion.5
  717.5 7.5 fusion.113
  728.3 3.4 fusion.110
  738.1 15.7 %scatter_custom_fusion.6 = f32[896,256]{1,0:T(8,128)} fusion(s32[2560]{0:T(1024)S(1)} %fusion.106, f32[2560,256]{1,0:T(8,128)} %bitcast.143, f32[]{:T(128)} %constant.105.clone.5..sunk), kind=kCustom, calls=%fused_computation.21.clone.1 | custom fusion | flops 655360 | bytes 918016 | tf_op jit(solution)/shard_map/while/body/eval_jaxpr/scatter-add | solution.py:150
  765.0 3.8 convert.9
  778.6 4.2 collective-permute-start.5
  784.5 30.8 %all-reduce = (f32[16,4]{0,1:T(4,128)}, f32[4]{0:T(128)}) all-reduce(f32[16,4]{0,1:T(4,128)S(1)} %fusion.22, f32[4]{0:T(128)S(1)} %select_reduce_fusion), channel_id=1, replica_groups=mesh['groups'=2,'atoms'=8,'samples'=2] {'atoms','samples'}, use_global_device_ids=true, to_apply=%region_9.10 | all-reduce | flops 68 | bytes 544 | tf_op jit(solution)/shard_map/psum | solution.py:181
  829.2 7.8 copy.54
  837.1 4.4 fusion.42
  842.3 5.1 convolution_convert_fusion
  850.1 91.1 %all-reduce.7.cloned.1.call-done = (f32[1,128,128]{2,1,0:T(8,128)}, f32[4,128,128]{2,1,0:T(8,128)}) async-done(((f32[1,128,128]{2,1,0:T(8,128)}, f32[4,128,128]{2,1,0:T(8,128)}), (f32[1,128,128]{2,1,0:T(8,128)}, f32[4,128,128]{2,1,0:T(8,128)})) %all-reduce.7.cloned.1.call-update) | async-done | bytes 327696 | tf_op jit(solution)/shard_map/psum | solution.py:181
  (406 shorter events, 375.3 us)
Async XLA Ops:
  7.2 65.5 %copy-start = (bf16[20,32,16,128]{3,2,1,0:T(8,128)(2,1)S(1)}, bf16[20,32,16,128]{3,2,1,0:T(8,128)(2,1)}, u32[]{:S(2)}) copy-start(bf16[20,32,16,128]{3,2,1,0:T(8,128)(2,1)} %param.21) | copy-start | bytes 7864324
  7.2 840.3 %all-reduce.5.cloned.1.call-start = ((), (), s32[]{:S(2)}) async-start(), calls=%async_computation | async-start | bytes 1310720 | tf_op jit(solution)/shard_map/psum | solution.py:189
  33.9 15.4 %copy-start.9 = (bf16[8,640,512]{2,1,0:T(8,128)(2,1)}, bf16[8,640,512]{2,1,0:T(8,128)(2,1)S(1)}, u32[]{:S(2)}) copy-start(bf16[8,640,512]{2,1,0:T(8,128)(2,1)S(1)} %convert.8) | copy-start | bytes 15728644
  33.9 8.6 copy-start.16
  35.1 39.5 %collective-permute-start.2 = (bf16[8,128,256]{2,1,0:T(8,128)(2,1)}, bf16[8,128,256]{2,1,0:T(8,128)(2,1)S(1)}, u32[]{:S(2)}, u32[]{:S(2)}) collective-permute-start(bf16[8,128,256]{2,1,0:T(8,128)(2,1)} %get-tuple-element.218), channel_id=1, source_target_pairs={{0,2},{2,4},{4,6},{6,8},{8,10},{10,12},{12,14},{1,3},{3,5},{5,7},{... | collective-permute-start | bytes 1572872 | tf_op jit(solution)/shard_map/ppermute | solution.py:18
  38.4 36.1 %collective-permute-start.3 = (bf16[8,128,256]{2,1,0:T(8,128)(2,1)}, bf16[8,128,256]{2,1,0:T(8,128)(2,1)}, u32[]{:S(2)}, u32[]{:S(2)}) collective-permute-start(bf16[8,128,256]{2,1,0:T(8,128)(2,1)} %get-tuple-element.219), channel_id=1, source_target_pairs={{2,0},{4,2},{6,4},{8,6},{10,8},{12,10},{14,12},{3,1},{5,3},{7,5},{... | collective-permute-start | bytes 1572872 | tf_op jit(solution)/shard_map/ppermute | solution.py:19
  42.5 18.7 %collective-permute-start = (s32[128]{0:T(128)S(1)}, s32[128]{0:T(128)S(1)}, u32[]{:S(2)}, u32[]{:S(2)}) collective-permute-start(s32[128]{0:T(128)S(1)} %get-tuple-element.226), channel_id=1, source_target_pairs={{0,2},{2,4},{4,6},{6,8},{8,10},{10,12},{12,14},{1,3},{3,5},{5,7},{... | collective-permute-start | bytes 1544 | tf_op jit(solution)/shard_map/ppermute | solution.py:18
  45.0 18.1 %collective-permute-start.1 = (s32[128]{0:T(128)S(1)}, s32[128]{0:T(128)S(1)}, u32[]{:S(2)}, u32[]{:S(2)}) collective-permute-start(s32[128]{0:T(128)S(1)} %get-tuple-element.227), channel_id=1, source_target_pairs={{2,0},{4,2},{6,4},{8,6},{10,8},{12,10},{14,12},{3,1},{5,3},{7,5},{... | collective-permute-start | bytes 1544 | tf_op jit(solution)/shard_map/ppermute | solution.py:19
  50.6 3.5 copy-start.19
  50.6 3.6 copy-start.15
  63.1 9.6 %copy-start.17 = (bf16[16,4]{0,1:T(4,128)(2,1)S(1)}, bf16[16,4]{0,1:T(4,128)(2,1)}, u32[]{:S(2)}) copy-start(bf16[16,4]{0,1:T(4,128)(2,1)} %param.27) | copy-start | bytes 388
  63.1 9.6 %copy-start.18 = (f32[4]{0:T(128)S(1)}, f32[4]{0:T(128)}, u32[]{:S(2)}) copy-start(f32[4]{0:T(128)} %param.28) | copy-start | bytes 52
  73.3 2.2 slice-start
  94.6 2.2 copy-start.1
  99.7 7.5 copy-start.10
  111.6 5.2 copy-start.5
  127.6 3.1 copy-start.2
  155.1 2.2 copy-start.3
  180.0 2.2 copy-start.1
  185.2 7.5 copy-start.10
  197.1 5.2 copy-start.5
  213.1 3.4 copy-start.2
  241.0 2.3 copy-start.3
  265.9 2.2 copy-start.1
  268.1 1.6 copy-start.4
  271.1 7.5 copy-start.10
  283.0 5.2 copy-start.5
  299.0 3.4 copy-start.2
  326.8 2.2 copy-start.3
  351.8 2.2 copy-start.1
  356.9 7.5 copy-start.10
  368.8 5.2 copy-start.5
  384.9 3.4 copy-start.2
  412.7 2.2 copy-start.3
  437.6 2.2 copy-start.1
  439.8 1.6 copy-start.4
  442.8 7.5 copy-start.10
  454.7 5.2 copy-start.5
  470.7 3.4 copy-start.2
  498.5 2.2 copy-start.3
  523.5 2.2 copy-start.1
  528.6 7.5 copy-start.10
  540.5 5.2 copy-start.5
  556.6 3.4 copy-start.2
  584.4 2.3 copy-start.3
  609.4 2.2 copy-start.1
  614.5 7.5 copy-start.10
  626.4 5.2 copy-start.5
  642.4 3.4 copy-start.2
  670.3 2.2 copy-start.3
  695.2 2.2 copy-start.1
  697.4 1.6 copy-start.4
  700.4 7.5 copy-start.10
  712.3 5.2 copy-start.5
  728.3 3.4 copy-start.2
  756.1 2.2 copy-start.3
  765.0 9.1 copy-start.8
  768.8 3.8 copy-start.6
  770.0 48.2 %collective-permute-start.4 = (bf16[8,128,256]{1,2,0:T(8,128)(2,1)}, bf16[8,128,256]{1,2,0:T(8,128)(2,1)S(1)}, u32[]{:S(2)}, u32[]{:S(2)}) collective-permute-start(bf16[8,128,256]{1,2,0:T(8,128)(2,1)} %get-tuple-element.221), channel_id=1, source_target_pairs={{0,2},{2,4},{4,6},{6,8},{8,10},{10,12},{12,14},{1,3},{3,5},{5,7},{... | collective-permute-start | bytes 1572872 | tf_op jit(solution)/shard_map/ppermute | solution.py:27
  778.6 42.0 %collective-permute-start.5 = (bf16[8,128,256]{1,2,0:T(8,128)(2,1)}, bf16[8,128,256]{1,2,0:T(8,128)(2,1)}, u32[]{:S(2)}, u32[]{:S(2)}) collective-permute-start(bf16[8,128,256]{1,2,0:T(8,128)(2,1)} %get-tuple-element.220), channel_id=1, source_target_pairs={{2,0},{4,2},{6,4},{8,6},{10,8},{12,10},{14,12},{3,1},{5,3},{7,5},{... | collective-permute-start | bytes 1572872 | tf_op jit(solution)/shard_map/ppermute | solution.py:27
  782.9 158.3 %all-reduce.7.cloned.1.call-start = ((), (), s32[]{:S(2)}) async-start(), calls=%async_computation.1 | async-start | bytes 655360 | tf_op jit(solution)/shard_map/psum | solution.py:181
  823.2 2.9 copy-start.11
  823.2 3.3 copy-start.12
  837.1 5.3 copy-start.14
  (14 other events, 19.0 us)
Sparse Core Ops, SparseCore 0:
  783.0 19.4 all-reduce.4
  847.6 93.5 all-reduce.6
where the time goes:
time: 956 us; the launch traced here: 950 us
  local copies, waits for them, and re-layouts  353 us (37%)
  other arithmetic  235 us (25%)
  matrix products  198 us (21%)
  waiting for transfers between devices  96.7 us (10%)
  blocking collectives  30.8 us (3%)
  starting transfers between devices  20.3 us (2%)
  between operations  15 us (2%)
    scatter-add x8, other arithmetic, one_sample(): jnp.zeros(sample_kv.shape, jnp.float32).at[key_rows].add(d_windowed)  125 us
    psum x1, waiting for transfers between devices, per_device(): lax.psum((weight_part, out_part, pair_weight_part, token_part), ('atoms',...  91.1 us
    dynamic_update_slice x48, local copies, waits for them, and re-layouts, per_device(): lax.scan(one_sample, jnp.zeros(pair_bias.shape, jnp.float32), (query, wid...  71.6 us
    gather x8, local copies, waits for them, and re-layouts, one_sample(): windowed = sample_kv[key_rows]  65.1 us
    dot_general x8, matrix products, attend(): jnp.einsum('whij,wjhd->wihd', probs_b, value_heads, preferred_element_typ...  60.3 us
    dot_general x8, matrix products, attend(): jnp.einsum('whij,wihd->wjhd', probs_b, attended_heads, preferred_element_...  59.8 us
    psum x1, blocking collectives, per_device(): lax.psum((weight_part, out_part, pair_weight_part, token_part), ('atoms',...  30.8 us
    while x128, local copies, waits for them, and re-layouts  28 us
  transfers between devices with their start and end apart: 8, of which 3 were waited for; matrix products, arithmetic and copies ran while one was open for 6% of the time, Pallas kernels for 0%

commit v1 on v0

v1 whole, which is shorter than its diff:
```python
import math

import jax
import jax.numpy as jnp
from jax import lax
from jax.experimental import pallas as pl
from jax.experimental.pallas import tpu as pltpu
from jax.sharding import PartitionSpec as P

MASKED = -1000000000.0
BF16 = jnp.bfloat16
F32 = jnp.float32


def nn(a, b):
    return lax.dot_general(a, b, (((1,), (0,)), ((), ())), preferred_element_type=F32)


def nt(a, b):
    return lax.dot_general(a, b, (((1,), (1,)), ((), ())), preferred_element_type=F32)


def tn(a, b):
    return lax.dot_general(a, b, (((0,), (0,)), ((), ())), preferred_element_type=F32)


def attention_kernel(
    heads,
    together,
    starts_ref,
    half_ref,
    act_ref,
    before_ref,
    after_ref,
    grad_ref,
    pair_ref,
    w_ref,
    wpair_ref,
    wtoken_ref,
    key_code_ref,
    query_code_ref,
    ga_ref,
    to_lower_ref,
    to_upper_ref,
    mine_ref,
    theirs_ref,
    sums_ref,
    wide_act,
    k_scr,
    v_scr,
    dk_scr,
    dv_scr,
    q_scr,
    gate_scr,
    gy_scr,
    dq_scr,
    dg_scr,
    gated_scr,
    pw_scr,
    tok_scr,
    bias_scr,
    ds_scr,
):
    samples, atoms, channels = act_ref.shape
    windows = pair_ref.shape[0]
    rows = atoms // windows
    halo = before_ref.shape[1]
    wide = atoms + 2 * halo
    span = halo
    head_dim = channels // heads
    scale = 1.0 / math.sqrt(head_dim)
    stack = heads * rows

    def project(s, carry):
        wide_act[s, 0:halo, :] = before_ref[s]
        wide_act[s, halo : halo + atoms, :] = act_ref[s]
        wide_act[s, halo + atoms : wide, :] = after_ref[s]
        full = wide_act[s]
        k_scr[s] = nn(full, w_ref[1]).astype(BF16).astype(F32)
        v_scr[s] = nn(full, w_ref[2]).astype(BF16).astype(F32)
        own = act_ref[s]
        q_scr[s] = nn(own, w_ref[0]).astype(BF16)
        gate_scr[s] = jax.nn.sigmoid(nn(own, w_ref[3]))
        gy_scr[s] = nt(grad_ref[s], w_ref[4])
        dk_scr[s] = jnp.zeros((wide, channels), F32)
        dv_scr[s] = jnp.zeros((wide, channels), F32)
        return carry

    lax.fori_loop(0, samples, project, 0)
    pw_scr[...] = jnp.zeros_like(pw_scr)
    tok_scr[...] = jnp.zeros_like(tok_scr)

    lane = lax.broadcasted_iota(jnp.int32, (rows, channels), 1) // head_dim
    head_is = [lane == h for h in range(heads)]

    def spread(x):
        wide_x = x.astype(F32)
        return jnp.concatenate(
            [jnp.where(head_is[h], wide_x, 0.0).astype(BF16) for h in range(heads)], axis=0
        )

    def collect(x):
        out = x[0:rows]
        for h in range(1, heads):
            out = jnp.where(head_is[h], x[h * rows : (h + 1) * rows], out)
        return out

    def window(w, carry):
        start = starts_ref[w]
        mine_rows = pl.ds(pl.multiple_of(w * rows, rows), rows)
        key_rows = pl.ds(start, span)
        key_code = key_code_ref[key_rows, :]
        same = key_code == query_code_ref[w]
        bias = tn(pair_ref[w], wpair_ref[...]) + jnp.where(same, wtoken_ref[...], 0.0)
        bias_scr[...] = jnp.where(key_code > 0.0, bias, MASKED)
        ds_scr[...] = jnp.zeros_like(ds_scr)

        def group(g, inner):
            ids = [g * together + u for u in range(together)]
            keys = [k_scr[s, key_rows, :].astype(BF16) for s in ids]
            values = [v_scr[s, key_rows, :].astype(BF16) for s in ids]
            qm = [spread(q_scr[s, mine_rows, :]) for s in ids]
            scores = [nt(k, q) * scale + bias_scr[...] for k, q in zip(keys, qm)]
            tops = [jnp.max(x, axis=0, keepdims=True) for x in scores]
            exps = [jnp.exp(x - t) for x, t in zip(scores, tops)]
            probs = [e * (1.0 / jnp.sum(e, axis=0, keepdims=True)) for e in exps]
            probs_b = [p.astype(BF16) for p in probs]
            attended = [collect(tn(p, v)) for p, v in zip(probs_b, values)]
            dam = []
            for s, a in zip(ids, attended):
                gate = gate_scr[s, mine_rows, :]
                gy = gy_scr[s, mine_rows, :]
                gated_scr[s, mine_rows, :] = (gate * a).astype(BF16)
                dg_scr[s, mine_rows, :] = (gy * a * gate * (1.0 - gate)).astype(BF16)
                dam.append(spread((gy * gate).astype(BF16)))
            dprobs = [nt(v, d) for v, d in zip(values, dam)]
            ds = [
                p * (d - jnp.sum(p * d, axis=0, keepdims=True)) for p, d in zip(probs, dprobs)
            ]
            ds_b = [d.astype(BF16) for d in ds]
            total = ds[0]
            for d in ds[1:]:
                total = total + d
            ds_scr[...] += total
            for i, s in enumerate(ids):
                dq_scr[s, mine_rows, :] = (collect(tn(ds_b[i], keys[i])) * scale).astype(BF16)
            for i, s in enumerate(ids):
                dk_scr[s, key_rows, :] += nn(ds_b[i], qm[i])
                dv_scr[s, key_rows, :] += nn(probs_b[i], dam[i])
            return inner

        lax.fori_loop(0, samples // together, group, 0)
        total = ds_scr[...]
        tok_scr[...] += jnp.where(same, total, 0.0)
        pw_scr[...] += nn(pair_ref[w], total.astype(BF16))
        turned = total.T
        half = rows // 2
        first_mine = half_ref[0] == 0
        for h in range(heads):
            low = turned[h * rows : h * rows + half]
            high = turned[h * rows + half : (h + 1) * rows]
            mine_ref[w, h * half : (h + 1) * half, :] = jnp.where(first_mine, low, high)
            theirs_ref[w, h * half : (h + 1) * half, :] = jnp.where(
                first_mine, high, low
            ).astype(BF16)
        return carry

    lax.fori_loop(0, windows, window, 0)

    sums_ref[...] = jnp.zeros_like(sums_ref)

    def finish(s, carry):
        dk = (dk_scr[s] * scale).astype(BF16)
        dv = dv_scr[s].astype(BF16)
        dq = dq_scr[s]
        dg = dg_scr[s]
        from_kv = nt(dk, w_ref[1]) + nt(dv, w_ref[2])
        to_lower_ref[s] = from_kv[0:halo].astype(BF16)
        to_upper_ref[s] = from_kv[halo + atoms : wide].astype(BF16)
        ga_ref[s] = from_kv[halo : halo + atoms] + nt(dq, w_ref[0]) + nt(dg, w_ref[3])
        own = act_ref[s]
        full = wide_act[s]
        c = channels
        sums_ref[0:c, :] += tn(own, dq)
        sums_ref[c : 2 * c, :] += tn(full, dk)
        sums_ref[2 * c : 3 * c, :] += tn(full, dv)
        sums_ref[3 * c : 4 * c, :] += tn(own, dg)
        sums_ref[4 * c : 5 * c, :] += tn(gated_scr[s], grad_ref[s])
        return carry

    lax.fori_loop(0, samples, finish, 0)
    pair_channels = pw_scr.shape[0] // rows
    shape = pw_scr.shape
    at_row = lax.broadcasted_iota(jnp.int32, shape, 0) // pair_channels
    at_col = lax.broadcasted_iota(jnp.int32, shape, 1) % rows
    diagonal = jnp.where(at_row == at_col, pw_scr[...], 0.0)
    base = 5 * channels
    sums_ref[base : base + pair_channels, :] = jnp.sum(
        diagonal.reshape(rows, pair_channels, stack), axis=0
    )
    sums_ref[base + pair_channels : base + pair_channels + 1, :] = jnp.sum(
        tok_scr[...], axis=0, keepdims=True
    )


def pair_kernel(mine_ref, got_ref, wt_ref, out_ref):
    def one(w, carry):
        total = mine_ref[w] + got_ref[w].astype(F32)
        high = total.astype(BF16)
        low = (total - high.astype(F32)).astype(BF16)
        weight = wt_ref[...]
        out_ref[w] = (nn(weight, high) + nn(weight, low)).astype(BF16)
        return carry

    lax.fori_loop(0, mine_ref.shape[0], one, 0)


def per_device(
    act,
    grad_out,
    pair,
    w_query,
    w_key,
    w_value,
    w_gate,
    w_out,
    w_pair,
    w_token,
    offsets,
    atom_token,
    padding,
):
    samples, atoms, channels = act.shape
    windows = offsets.shape[0]
    rows = atoms // windows
    pair_channels, heads = w_pair.shape
    span = pair.shape[-1]
    stack = heads * rows
    half = rows // 2
    ranges = lax.axis_size("atoms")
    wide = atoms + 2 * span
    up = [(i, i + 1) for i in range(ranges - 1)]
    down = [(i + 1, i) for i in range(ranges - 1)]

    before = lax.ppermute(act[:, atoms - span :], "atoms", up)
    after = lax.ppermute(act[:, :span], "atoms", down)
    position = jnp.arange(atoms, dtype=jnp.int32)
    codes = jnp.where(position < atoms - padding[0], atom_token + 1, 0)
    code_before = lax.ppermute(codes[atoms - span :], "atoms", up)
    code_after = lax.ppermute(codes[:span], "atoms", down)
    wide_codes = jnp.concatenate([code_before, codes, code_after]).astype(F32)
    key_code = jnp.broadcast_to(wide_codes[:, None], (wide, stack))
    query_code = jnp.tile((atom_token + 1).astype(F32).reshape(windows, 1, rows), (1, 1, heads))
    anchor = lax.axis_index("atoms") * atoms
    starts = (
        jnp.clip(
            anchor + rows * jnp.arange(windows, dtype=jnp.int32) + offsets,
            0,
            ranges * atoms - span,
        )
        - anchor
        + span
    )
    me = lax.axis_index("samples").astype(jnp.int32)
    eye = jnp.eye(rows, dtype=BF16)
    wpair_big = (eye[:, None, None, :] * w_pair[None, :, :, None]).reshape(
        rows * pair_channels, stack
    )
    eye_half = jnp.eye(half, dtype=BF16)
    wpair_half = (eye_half[:, None, None, :] * w_pair[None, :, :, None]).reshape(
        half * pair_channels, heads * half
    )
    wtoken_row = jnp.repeat(w_token, rows)[None, :]
    weights = jnp.stack([w_query, w_key, w_value, w_gate, w_out])

    together = 4 if samples % 4 == 0 else 1
    vmem = pl.BlockSpec(memory_space=pltpu.VMEM)
    smem = pl.BlockSpec(memory_space=pltpu.SMEM)
    sum_rows = 5 * channels + pair_channels + 8

    def kernel(*refs):
        attention_kernel(heads, together, *refs)

    ga, to_lower, to_upper, mine, theirs, sums = pl.pallas_call(
        kernel,
        out_shape=(
            jax.ShapeDtypeStruct((samples, atoms, channels), F32),
            jax.ShapeDtypeStruct((samples, span, channels), BF16),
            jax.ShapeDtypeStruct((samples, span, channels), BF16),
            jax.ShapeDtypeStruct((windows, heads * half, span), F32),
            jax.ShapeDtypeStruct((windows, heads * half, span), BF16),
            jax.ShapeDtypeStruct((sum_rows, channels), F32),
        ),
        in_specs=[smem, smem] + [vmem] * 10,
        out_specs=(vmem,) * 6,
        scratch_shapes=[
            pltpu.VMEM((samples, wide, channels), BF16),
            pltpu.VMEM((samples, wide, channels), F32),
            pltpu.VMEM((samples, wide, channels), F32),
            pltpu.VMEM((samples, wide, channels), F32),
            pltpu.VMEM((samples, wide, channels), F32),
            pltpu.VMEM((samples, atoms, channels), BF16),
            pltpu.VMEM((samples, atoms, channels), F32),
            pltpu.VMEM((samples, atoms, channels), F32),
            pltpu.VMEM((samples, atoms, channels), BF16),
            pltpu.VMEM((samples, atoms, channels), BF16),
            pltpu.VMEM((samples, atoms, channels), BF16),
            pltpu.VMEM((rows * pair_channels, stack), F32),
            pltpu.VMEM((span, stack), F32),
            pltpu.VMEM((span, stack), F32),
            pltpu.VMEM((span, stack), F32),
        ],
        compiler_params=pltpu.CompilerParams(vmem_limit_bytes=56 * 1024 * 1024),
        name="attention",
    )(
        starts,
        me.reshape(1),
        act,
        before,
        after,
        grad_out,
        pair.reshape(windows, rows * pair_channels, span),
        weights,
        wpair_big,
        wtoken_row,
        key_code,
        query_code,
    )

    from_upper = lax.ppermute(to_lower, "atoms", down).astype(F32)
    from_lower = lax.ppermute(to_upper, "atoms", up).astype(F32)
    count = lax.axis_size("samples")
    got = lax.ppermute(theirs, "samples", [(i, (i + 1) % count) for i in range(count)])
    total = lax.psum(sums, ("atoms", "samples"))

    grad_act = jnp.concatenate(
        [
            ga[:, :span] + from_lower,
            ga[:, span : atoms - span],
            ga[:, atoms - span :] + from_upper,
        ],
        axis=1,
    ).astype(BF16)
    grad_pair = pl.pallas_call(
        pair_kernel,
        out_shape=jax.ShapeDtypeStruct((windows, half * pair_channels, span), BF16),
        in_specs=[vmem] * 3,
        out_specs=vmem,
        name="pair_grad",
    )(mine, got, wpair_half).reshape(windows, half, pair_channels, span)

    base = 5 * channels
    grad_weights = total[:base].reshape(5, channels, channels)
    grad_pair_weight = jnp.sum(
        total[base : base + pair_channels].reshape(pair_channels, heads, rows), axis=-1
    )
    grad_token_weight = jnp.sum(total[base + pair_channels].reshape(heads, rows), axis=-1)
    return (grad_act, grad_pair, grad_weights, grad_pair_weight, grad_token_weight)


def solution(mesh):
    in_specs = (
        P("samples", ("groups", "atoms"), None),
        P("samples", ("groups", "atoms"), None),
        P(("groups", "atoms"), None, None, None),
        P(),
        P(),
        P(),
        P(),
        P(),
        P(),
        P(),
        P(("groups", "atoms")),
        P(("groups", "atoms")),
        P(("groups", "atoms")),
    )
    out_specs = (
        P("samples", ("groups", "atoms"), None),
        P(("groups", "atoms"), "samples", None, None),
        P("groups", None, None),
        P("groups", None),
        P("groups"),
    )
    return jax.shard_map(
        per_device, mesh=mesh, in_specs=in_specs, out_specs=out_specs, check_vma=False
    )
```

time: 956 us -> 206 us (0.22)
  local copies, waits for them, and re-layouts: 353 us -> 14.8 us
  other arithmetic: 235 us -> 4.81 us
  matrix products: 198 us -> 0 us
  Pallas kernels: 0 us -> 59.7 us
  blocking collectives: 30.8 us -> 0 us
    dot_general x56 -> x0, matrix products: 198 us -> none  [the longest x8 60.3 us: attend(): jnp.einsum('whij,wjhd->wihd', probs_b, value_heads, preferred_element_typ...]
    scatter-add x10 -> x0, other arithmetic: 130 us -> none  [the longest x8 125 us: one_sample(): jnp.zeros(sample_kv.shape, jnp.float32).at[key_rows].add(d_windowed)]
    gather x9 -> x0, local copies, waits for them, and re-layouts: 74.5 us -> none  [the longest x8 65.1 us: one_sample(): windowed = sample_kv[key_rows]]
    dynamic_update_slice x48 -> x0, local copies, waits for them, and re-layouts: 71.6 us -> none  [per_device(): lax.scan(one_sample, jnp.zeros(pair_bias.shape, jnp.float32), (query, wid...]
    pallas_call x0 -> x2, Pallas kernels: none -> 59.7 us  [the longest x1 54 us: per_device(): pl.pallas_call(kernel, out_shape=(jax.ShapeDtypeStruct((samples, atoms, c...]
    reshape x26 -> x1, local copies, waits for them, and re-layouts: 47.5 us -> 0.08 us  [per_device(): total[base:base + pair_channels].reshape(pair_channels, heads, rows)]
    convert_element_type x17 -> x4, other arithmetic: 46.1 us -> 0.72 us  [the longest x1 0.69 us: per_device(): (atom_token + 1).astype(F32).reshape(windows, 1, rows)]
    concatenate x10 -> x0, local copies, waits for them, and re-layouts: 35.3 us -> none  [the longest x8 26.6 us: one_sample(): jnp.concatenate([d_keys.reshape(windows, key_span, channels), d_values.re...]
  transfers between devices with their start and end apart: 8 -> 8, of which waited for: 3 -> 2; matrix products, arithmetic and copies ran while one was open for 6% -> 8% of each run, Pallas kernels for 0% -> 0%
where the time goes in v1:
time: 206 us; the launch traced here: 205 us
  waiting for transfers between devices  90.8 us (44%)
  Pallas kernels  59.7 us (29%)
  starting transfers between devices  20.4 us (10%)
  between operations  14.9 us (7%)
  local copies, waits for them, and re-layouts  14.8 us (7%)
  other arithmetic  4.81 us (2%)
    psum x1, waiting for transfers between devices, per_device(): total = lax.psum(sums, ('atoms', 'samples'))  88.1 us
    pallas_call x1, Pallas kernels, per_device(): pl.pallas_call(kernel, out_shape=(jax.ShapeDtypeStruct((samples, atoms, c...  54 us
    pallas_call x1, Pallas kernels, per_device(): pl.pallas_call(pair_kernel, out_shape=jax.ShapeDtypeStruct((windows, half...  5.74 us
    ppermute x1, starting transfers between devices, per_device(): from_upper = lax.ppermute(to_lower, 'atoms', down).astype(F32)  4.82 us
    unnamed x26, local copies, waits for them, and re-layouts  4.48 us
    ppermute x1, starting transfers between devices, per_device(): after = lax.ppermute(act[:, :span], 'atoms', down)  4.24 us
  transfers between devices with their start and end apart: 8, of which 2 were waited for; matrix products, arithmetic and copies ran while one was open for 8% of the time, Pallas kernels for 0%

profile of v1, /device:TPU:8, one launch (start us, length us, event | category | flops | bytes accessed | tf_op | source)
XLA Modules:
  0.0 205.4 jit_solution(585213232792045007)
XLA Ops:
  7.2 0.0 copy-start.4
  7.2 0.0 copy-start.5
  7.2 0.0 copy-start.9
  7.2 0.0 all-reduce.2.cloned.1.call-start
  7.9 0.7 add_convert_fusion.3
  8.6 3.4 %collective-permute-start.2 = (s32[128]{0:T(128)S(1)}, s32[128]{0:T(128)S(1)}, u32[]{:S(2)}, u32[]{:S(2)}) collective-permute-start(s32[128]{0:T(128)S(1)} %get-tuple-element.28), channel_id=1, source_target_pairs={{0,2},{2,4},{4,6},{6,8},{8,10},{10,12},{12,14},{1,3},{3,5},{5,7},{... | collective-permute-start | bytes 1544 | tf_op jit(solution)/shard_map/ppermute | solution.py:249
  12.0 0.0 copy-start.7
  12.0 3.3 %collective-permute-start.3 = (s32[128]{0:T(128)S(1)}, s32[128]{0:T(128)S(1)}, u32[]{:S(2)}, u32[]{:S(2)}) collective-permute-start(s32[128]{0:T(128)S(1)} %get-tuple-element.29), channel_id=1, source_target_pairs={{2,0},{4,2},{6,4},{8,6},{10,8},{12,10},{14,12},{3,1},{5,3},{7,5},{... | collective-permute-start | bytes 1544 | tf_op jit(solution)/shard_map/ppermute | solution.py:250
  15.3 1.1 fusion.3
  16.4 2.5 %collective-permute-start = (bf16[8,128,128]{2,1,0:T(8,128)(2,1)S(1)}, bf16[8,128,128]{2,1,0:T(8,128)(2,1)S(1)}, u32[]{:S(2)}, u32[]{:S(2)}) collective-permute-start(bf16[8,128,128]{2,1,0:T(8,128)(2,1)S(1)} %get-tuple-element.25), channel_id=1, source_target_pairs={{0,2},{2,4},{4,6},{6,8},{8,10},{10,12},{12,14},{1,3},{3,5},{5,7},{... | collective-permute-start | bytes 786440 | tf_op jit(solution)/shard_map/ppermute | solution.py:245
  18.9 4.2 %collective-permute-start.1 = (bf16[8,128,128]{2,1,0:T(8,128)(2,1)S(1)}, bf16[8,128,128]{2,1,0:T(8,128)(2,1)S(1)}, u32[]{:S(2)}, u32[]{:S(2)}) collective-permute-start(bf16[8,128,128]{2,1,0:T(8,128)(2,1)S(1)} %get-tuple-element.24), channel_id=1, source_target_pairs={{2,0},{4,2},{6,4},{8,6},{10,8},{12,10},{14,12},{3,1},{5,3},{7,5},{... | collective-permute-start | bytes 786440 | tf_op jit(solution)/shard_map/ppermute | solution.py:246
  23.2 0.8 bitcast_dynamic-update-slice_fusion.4
  24.0 0.8 copy.22
  24.7 0.8 bitcast_dynamic-update-slice_fusion.3
  25.5 0.8 bitcast_dynamic-update-slice_fusion.2
  26.3 0.0 copy-done.4
  26.3 0.0 copy-done.5
  26.3 0.0 copy-start.3
  26.3 0.3 broadcast_multiply_fusion
  26.6 0.0 copy-done.9
  26.6 0.5 subtract_add_fusion.refs_0_
  27.1 0.1 tile.10
  27.2 0.7 tile.12.refs_11_
  27.9 0.9 mul.45.refs_8_
  28.8 0.0 copy-done.7
  28.8 0.1 broadcast_in_dim.8
  28.9 0.7 broadcast_in_dim_reshape.3.refs_9_
  29.6 0.0 collective-permute-done.2
  29.6 0.0 collective-permute-done.3
  29.6 0.0 collective-permute-done.refs_3_
  29.6 0.0 copy-start.1
  29.6 2.7 %collective-permute-done.1.refs_4_ = bf16[8,128,128]{2,1,0:T(8,128)(2,1)S(1)} collective-permute-done((bf16[8,128,128]{2,1,0:T(8,128)(2,1)S(1)}, bf16[8,128,128]{2,1,0:T(8,128)(2,1)S(1)}, u32[]{:S(2)}, u32[]{:S(2)}) %collective-permute-start.1) | collective-permute-done | bytes 262176 | tf_op jit(solution)/shard_map/ppermute | solution.py:246
  32.3 0.0 copy-start.2
  32.3 1.0 broadcast_in_dim.10.refs_10_
  33.3 0.0 copy-done.3
  33.3 0.0 copy-done.1
  33.3 0.0 copy-done.2
  33.3 54.0 %attention.1 = (f32[8,640,128]{2,1,0:T(8,128)}, bf16[8,128,128]{2,1,0:T(8,128)(2,1)}, bf16[8,128,128]{2,1,0:T(8,128)(2,1)}, f32[20,64,128]{2,1,0:T(8,128)}, bf16...) custom-call(s32[20]{0:T(128)} %subtract_add_fusion.refs_0_, s32[1]{0:T(128)} %bitcast.refs_1_, bf16[8,640,128]{2,1,0:T(8,128)(2,1)} %refs_2_.1, ...), custom_call_target="tpu_custom_call" | custom-call | tf_op jit(solution)/shard_map/attention/pallas_call | solution.py:284
  87.3 2.0 collective-permute-start.4
  89.3 4.8 %collective-permute-start.5 = (bf16[8,128,128]{2,1,0:T(8,128)(2,1)}, bf16[8,128,128]{2,1,0:T(8,128)(2,1)S(1)}, u32[]{:S(2)}, u32[]{:S(2)}) collective-permute-start(bf16[8,128,128]{2,1,0:T(8,128)(2,1)} %get-tuple-element.13), channel_id=1, source_target_pairs={{2,0},{4,2},{6,4},{8,6},{10,8},{12,10},{14,12},{3,1},{5,3},{7,5},{... | collective-permute-start | bytes 786440 | tf_op jit(solution)/shard_map/ppermute | solution.py:330
  94.1 0.0 all-reduce.2.cloned.1.call-update
  94.2 0.0 copy-done.6
  94.2 0.1 broadcast_multiply_fusion.1
  94.3 0.2 mul.49
  94.5 0.7 copy.23.wt_ref
  95.2 1.5 slice.49
  96.8 0.0 copy-done.8
  96.8 0.1 collective-permute-start.6
  96.9 88.1 %all-reduce.2.cloned.1.call-done = f32[664,128]{1,0:T(8,128)} async-done(((f32[664,128]{1,0:T(8,128)}), f32[664,128]{1,0:T(8,128)}) %all-reduce.2.cloned.1.call-update) | async-done | bytes 339984 | tf_op jit(solution)/shard_map/psum | solution.py:334
  185.0 0.7 slice.43
  185.7 0.1 reshape.84
  185.7 0.1 reduce_sum.18
  185.8 0.7 copy.24
  186.5 0.7 slice_reduce_fusion
  187.2 0.1 reshape_squeeze.3
  187.3 0.6 reduce_sum.19
  187.9 1.7 slice.42
  189.6 0.0 collective-permute-done.4
  189.6 0.0 collective-permute-done.5
  189.6 1.3 add_convert_fusion.1
  191.0 1.1 pad_maximum_fusion
  192.1 0.0 collective-permute-done.6.got_ref
  192.1 0.7 copy-done
  192.9 5.7 %pair_grad.1 = bf16[20,256,128]{2,1,0:T(8,128)(2,1)} custom-call(f32[20,64,128]{2,1,0:T(8,128)} %get-tuple-element.14.mine_ref, bf16[20,64,128]{2,1,0:T(8,128)(2,1)} %copy-done, bf16[256,64]{1,0:T(8,128)(2,1)} %copy.23.wt_ref), custom_call_target="tpu_custom_call" | custom-call | tf_op jit(solution)/shard_map/pair_grad/pallas_call | solution.py:344
  (10 shorter events, 0.1 us)
Async XLA Ops:
  7.2 19.1 %copy-start.4 = (bf16[128,128]{1,0:T(8,128)(2,1)S(1)}, bf16[128,128]{1,0:T(8,128)(2,1)}, u32[]{:S(2)}) copy-start(bf16[128,128]{1,0:T(8,128)(2,1)} %param.19) | copy-start | bytes 98308
  7.2 19.1 %copy-start.5 = (bf16[128,128]{1,0:T(8,128)(2,1)S(1)}, bf16[128,128]{1,0:T(8,128)(2,1)}, u32[]{:S(2)}) copy-start(bf16[128,128]{1,0:T(8,128)(2,1)} %param.20) | copy-start | bytes 98308
  7.2 19.4 %copy-start.9 = (s32[20]{0:T(128)S(1)}, s32[20]{0:T(128)}, u32[]{:S(2)}) copy-start(s32[20]{0:T(128)} %param.23) | copy-start | bytes 244
  7.2 177.8 %all-reduce.2.cloned.1.call-start = ((), (), s32[]{:S(2)}) async-start(), calls=%async_computation | async-start | bytes 679936 | tf_op jit(solution)/shard_map/psum | solution.py:334
  8.6 21.0 %collective-permute-start.2 = (s32[128]{0:T(128)S(1)}, s32[128]{0:T(128)S(1)}, u32[]{:S(2)}, u32[]{:S(2)}) collective-permute-start(s32[128]{0:T(128)S(1)} %get-tuple-element.28), channel_id=1, source_target_pairs={{0,2},{2,4},{4,6},{6,8},{8,10},{10,12},{12,14},{1,3},{3,5},{5,7},{... | collective-permute-start | bytes 1544 | tf_op jit(solution)/shard_map/ppermute | solution.py:249
  12.0 16.9 %copy-start.7 = (f32[4]{0:T(128)S(1)}, f32[4]{0:T(128)}, u32[]{:S(2)}) copy-start(f32[4]{0:T(128)} %param.22) | copy-start | bytes 52
  12.0 17.6 %collective-permute-start.3 = (s32[128]{0:T(128)S(1)}, s32[128]{0:T(128)S(1)}, u32[]{:S(2)}, u32[]{:S(2)}) collective-permute-start(s32[128]{0:T(128)S(1)} %get-tuple-element.29), channel_id=1, source_target_pairs={{2,0},{4,2},{6,4},{8,6},{10,8},{12,10},{14,12},{3,1},{5,3},{7,5},{... | collective-permute-start | bytes 1544 | tf_op jit(solution)/shard_map/ppermute | solution.py:250
  16.4 13.2 %collective-permute-start = (bf16[8,128,128]{2,1,0:T(8,128)(2,1)S(1)}, bf16[8,128,128]{2,1,0:T(8,128)(2,1)S(1)}, u32[]{:S(2)}, u32[]{:S(2)}) collective-permute-start(bf16[8,128,128]{2,1,0:T(8,128)(2,1)S(1)} %get-tuple-element.25), channel_id=1, source_target_pairs={{0,2},{2,4},{4,6},{6,8},{8,10},{10,12},{12,14},{1,3},{3,5},{5,7},{... | collective-permute-start | bytes 786440 | tf_op jit(solution)/shard_map/ppermute | solution.py:245
  18.9 13.4 %collective-permute-start.1 = (bf16[8,128,128]{2,1,0:T(8,128)(2,1)S(1)}, bf16[8,128,128]{2,1,0:T(8,128)(2,1)S(1)}, u32[]{:S(2)}, u32[]{:S(2)}) collective-permute-start(bf16[8,128,128]{2,1,0:T(8,128)(2,1)S(1)} %get-tuple-element.24), channel_id=1, source_target_pairs={{2,0},{4,2},{6,4},{8,6},{10,8},{12,10},{14,12},{3,1},{5,3},{7,5},{... | collective-permute-start | bytes 786440 | tf_op jit(solution)/shard_map/ppermute | solution.py:246
  26.3 7.0 %copy-start.3 = (bf16[5,128,128]{2,1,0:T(8,128)(2,1)}, bf16[5,128,128]{2,1,0:T(8,128)(2,1)S(1)}, u32[]{:S(2)}) copy-start(bf16[5,128,128]{2,1,0:T(8,128)(2,1)S(1)} %bitcast_dynamic-update-slice_fusion.refs_7_) | copy-start | bytes 491524
  29.6 3.7 %copy-start.1 = (bf16[8,128,128]{2,1,0:T(8,128)(2,1)}, bf16[8,128,128]{2,1,0:T(8,128)(2,1)S(1)}, u32[]{:S(2)}) copy-start(bf16[8,128,128]{2,1,0:T(8,128)(2,1)S(1)} %collective-permute-done.refs_3_) | copy-start | bytes 786436
  32.3 1.0 copy-start.2
  33.3 60.9 %copy-start.6 = (bf16[16,4]{0,1:T(4,128)(2,1)S(1)}, bf16[16,4]{0,1:T(4,128)(2,1)}, u32[]{:S(2)}) copy-start(bf16[16,4]{0,1:T(4,128)(2,1)} %param.21) | copy-start | bytes 388
  87.2 9.5 %copy-start.8 = (bf16[20,64,128]{2,1,0:T(8,128)(2,1)S(1)}, bf16[20,64,128]{2,1,0:T(8,128)(2,1)}, u32[]{:S(2)}) copy-start(bf16[20,64,128]{2,1,0:T(8,128)(2,1)} %get-tuple-element.15) | copy-start | bytes 983044
  87.3 102.4 %collective-permute-start.4 = (bf16[8,128,128]{2,1,0:T(8,128)(2,1)}, bf16[8,128,128]{2,1,0:T(8,128)(2,1)S(1)}, u32[]{:S(2)}, u32[]{:S(2)}) collective-permute-start(bf16[8,128,128]{2,1,0:T(8,128)(2,1)} %get-tuple-element.12), channel_id=1, source_target_pairs={{0,2},{2,4},{4,6},{6,8},{8,10},{10,12},{12,14},{1,3},{3,5},{5,7},{... | collective-permute-start | bytes 786440 | tf_op jit(solution)/shard_map/ppermute | solution.py:331
  89.3 100.3 %collective-permute-start.5 = (bf16[8,128,128]{2,1,0:T(8,128)(2,1)}, bf16[8,128,128]{2,1,0:T(8,128)(2,1)S(1)}, u32[]{:S(2)}, u32[]{:S(2)}) collective-permute-start(bf16[8,128,128]{2,1,0:T(8,128)(2,1)} %get-tuple-element.13), channel_id=1, source_target_pairs={{2,0},{4,2},{6,4},{8,6},{10,8},{12,10},{14,12},{3,1},{5,3},{7,5},{... | collective-permute-start | bytes 786440 | tf_op jit(solution)/shard_map/ppermute | solution.py:330
  96.8 95.3 %collective-permute-start.6 = (bf16[20,64,128]{2,1,0:T(8,128)(2,1)S(1)}, bf16[20,64,128]{2,1,0:T(8,128)(2,1)S(1)}, u32[]{:S(2)}, u32[]{:S(2)}) collective-permute-start(bf16[20,64,128]{2,1,0:T(8,128)(2,1)S(1)} %copy-done.8), channel_id=1, source_target_pairs={{0,1},{1,0},{2,3},{3,2},{4,5},{5,4},{6,7},{7,6},{8,9},{9,8},{10,11... | collective-permute-start | bytes 983048 | tf_op jit(solution)/shard_map/ppermute | solution.py:333
  192.1 0.7 copy-start
Sparse Core Ops, SparseCore 0:
  94.3 90.6 all-reduce.1

commit v2 on v1

--- a/solution.py
+++ b/solution.py
@@ -27,17 +27,22 @@
 def attention_kernel(
     heads,
     together,
-    starts_ref,
-    half_ref,
+    offsets_ref,
+    wtoken_ref,
     act_ref,
     before_ref,
     after_ref,
     grad_ref,
     pair_ref,
-    w_ref,
+    wq_ref,
+    wk_ref,
+    wv_ref,
+    wg_ref,
+    wo_ref,
     wpair_ref,
-    wtoken_ref,
-    key_code_ref,
+    code_ref,
+    code_before_ref,
+    code_after_ref,
     query_code_ref,
     ga_ref,
     to_lower_ref,
@@ -60,6 +65,8 @@
     tok_scr,
     bias_scr,
     ds_scr,
+    key_code_scr,
+    wpair_scr,
 ):
     samples, atoms, channels = act_ref.shape
     windows = pair_ref.shape[0]
@@ -76,12 +83,12 @@
         wide_act[s, halo : halo + atoms, :] = act_ref[s]
         wide_act[s, halo + atoms : wide, :] = after_ref[s]
         full = wide_act[s]
-        k_scr[s] = nn(full, w_ref[1]).astype(BF16).astype(F32)
-        v_scr[s] = nn(full, w_ref[2]).astype(BF16).astype(F32)
+        k_scr[s] = nn(full, wk_ref[...]).astype(BF16).astype(F32)
+        v_scr[s] = nn(full, wv_ref[...]).astype(BF16).astype(F32)
         own = act_ref[s]
-        q_scr[s] = nn(own, w_ref[0]).astype(BF16)
-        gate_scr[s] = jax.nn.sigmoid(nn(own, w_ref[3]))
-        gy_scr[s] = nt(grad_ref[s], w_ref[4])
+        q_scr[s] = nn(own, wq_ref[...]).astype(BF16)
+        gate_scr[s] = jax.nn.sigmoid(nn(own, wg_ref[...]))
+        gy_scr[s] = nt(grad_ref[s], wo_ref[...])
         dk_scr[s] = jnp.zeros((wide, channels), F32)
         dv_scr[s] = jnp.zeros((wide, channels), F32)
         return carry
@@ -89,6 +96,32 @@
     lax.fori_loop(0, samples, project, 0)
     pw_scr[...] = jnp.zeros_like(pw_scr)
     tok_scr[...] = jnp.zeros_like(tok_scr)
+
+    def code_column(first, row):
+        column = jnp.broadcast_to(row.astype(F32), (stack, span)).T
+        key_code_scr[first : first + span, :] = column
+
+    code_column(0, code_before_ref[0])
+    for r in range(atoms // span):
+        code_column(halo + r * span, code_ref[r])
+    code_column(halo + atoms, code_after_ref[0])
+
+    pair_channels = wpair_ref.shape[0]
+    lane_head = lax.broadcasted_iota(jnp.int32, (pair_channels, stack), 1) // rows
+    wpair_values = wpair_ref[...].astype(F32)
+    wpair_rows = jnp.zeros((pair_channels, stack), F32)
+    wtoken_row = jnp.zeros((1, stack), F32)
+    for h in range(heads):
+        wpair_rows = jnp.where(lane_head == h, wpair_values[:, h : h + 1], wpair_rows)
+        wtoken_row = jnp.where(lane_head[0:1] == h, wtoken_ref[h], wtoken_row)
+    lane_row = lax.broadcasted_iota(jnp.int32, (pair_channels, stack), 1) % rows
+    for i in range(rows):
+        wpair_scr[i * pair_channels : (i + 1) * pair_channels, :] = jnp.where(
+            lane_row == i, wpair_rows, 0.0
+        ).astype(BF16)
+    anchor = lax.axis_index("atoms") * atoms
+    last_start = lax.axis_size("atoms") * atoms - span
+    first_mine = lax.axis_index("samples") == 0
 
     lane = lax.broadcasted_iota(jnp.int32, (rows, channels), 1) // head_dim
     head_is = [lane == h for h in range(heads)]
@@ -106,12 +139,12 @@
         return out
 
     def window(w, carry):
-        start = starts_ref[w]
+        start = jnp.clip(anchor + w * rows + offsets_ref[w], 0, last_start) - anchor + span
         mine_rows = pl.ds(pl.multiple_of(w * rows, rows), rows)
         key_rows = pl.ds(start, span)
-        key_code = key_code_ref[key_rows, :]
-        same = key_code == query_code_ref[w]
-        bias = tn(pair_ref[w], wpair_ref[...]) + jnp.where(same, wtoken_ref[...], 0.0)
+        key_code = key_code_scr[key_rows, :]
+        same = key_code == query_code_ref[w].astype(F32)
+        bias = tn(pair_ref[w], wpair_scr[...]) + jnp.where(same, wtoken_row, 0.0)
         bias_scr[...] = jnp.where(key_code > 0.0, bias, MASKED)
         ds_scr[...] = jnp.zeros_like(ds_scr)
 
@@ -155,7 +188,6 @@
         pw_scr[...] += nn(pair_ref[w], total.astype(BF16))
         turned = total.T
         half = rows // 2
-        first_mine = half_ref[0] == 0
         for h in range(heads):
             low = turned[h * rows : h * rows + half]
             high = turned[h * rows + half : (h + 1) * rows]
@@ -174,10 +206,10 @@
         dv = dv_scr[s].astype(BF16)
         dq = dq_scr[s]
         dg = dg_scr[s]
-        from_kv = nt(dk, w_ref[1]) + nt(dv, w_ref[2])
+        from_kv = nt(dk, wk_ref[...]) + nt(dv, wv_ref[...])
         to_lower_ref[s] = from_kv[0:halo].astype(BF16)
         to_upper_ref[s] = from_kv[halo + atoms : wide].astype(BF16)
-        ga_ref[s] = from_kv[halo : halo + atoms] + nt(dq, w_ref[0]) + nt(dg, w_ref[3])
+        ga_ref[s] = from_kv[halo : halo + atoms] + nt(dq, wq_ref[...]) + nt(dg, wg_ref[...])
         own = act_ref[s]
         full = wide_act[s]
         c = channels
@@ -189,7 +221,6 @@
         return carry
 
     lax.fori_loop(0, samples, finish, 0)
-    pair_channels = pw_scr.shape[0] // rows
     shape = pw_scr.shape
     at_row = lax.broadcasted_iota(jnp.int32, shape, 0) // pair_channels
     at_col = lax.broadcasted_iota(jnp.int32, shape, 1) % rows
@@ -203,16 +234,248 @@
     )
 
 
-def pair_kernel(mine_ref, got_ref, wt_ref, out_ref):
-    def one(w, carry):
-        total = mine_ref[w] + got_ref[w].astype(F32)
-        high = total.astype(BF16)
-        low = (total - high.astype(F32)).astype(BF16)
-        weight = wt_ref[...]
-        out_ref[w] = (nn(weight, high) + nn(weight, low)).astype(BF16)
+def greet(barrier, devices):
+    for device in devices:
+        pl.semaphore_signal(
+            barrier, inc=1, device_id=device, device_id_type=pl.DeviceIdType.MESH
+        )
+
+
+def remote(src, dst, sems, slot, device):
+    return pltpu.make_async_remote_copy(
+        src_ref=src,
+        dst_ref=dst,
+        send_sem=sems.at[0, slot],
+        recv_sem=sems.at[1, slot],
+        device_id=device,
+        device_id_type=pl.DeviceIdType.MESH,
+    )
+
+
+def halo_kernel(
+    ranges,
+    span,
+    act_ref,
+    code_ref,
+    before_ref,
+    after_ref,
+    code_before_ref,
+    code_after_ref,
+    sems,
+):
+    me = lax.axis_index("atoms")
+    atoms = act_ref.shape[1]
+    has_lower, has_upper = me > 0, me < ranges - 1
+    lower, upper = {"atoms": me - 1}, {"atoms": me + 1}
+    barrier = pltpu.get_barrier_semaphore()
+
+    @pl.when(has_lower)
+    def _():
+        greet(barrier, [lower])
+
+    @pl.when(has_upper)
+    def _():
+        greet(barrier, [upper])
+
+    inside = jnp.logical_and(has_lower, has_upper)
+
+    @pl.when(inside)
+    def _():
+        pl.semaphore_wait(barrier, 2)
+
+    @pl.when(jnp.logical_not(inside))
+    def _():
+        pl.semaphore_wait(barrier, 1)
+
+    last = code_ref.shape[0] - 1
+    to_upper = [
+        remote(act_ref.at[:, pl.ds(atoms - span, span)], before_ref, sems, 0, upper),
+        remote(code_ref.at[pl.ds(last, 1)], code_before_ref, sems, 1, upper),
+    ]
+    to_lower = [
+        remote(act_ref.at[:, pl.ds(0, span)], after_ref, sems, 2, lower),
+        remote(code_ref.at[pl.ds(0, 1)], code_after_ref, sems, 3, lower),
+    ]
+
+    @pl.when(has_upper)
+    def _():
+        for copy in to_upper:
+            copy.start()
+
+    @pl.when(has_lower)
+    def _():
+        for copy in to_lower:
+            copy.start()
+
+    @pl.when(jnp.logical_not(has_lower))
+    def _():
+        before_ref[...] = jnp.zeros_like(before_ref)
+        code_before_ref[...] = jnp.zeros_like(code_before_ref)
+
+    @pl.when(jnp.logical_not(has_upper))
+    def _():
+        after_ref[...] = jnp.zeros_like(after_ref)
+        code_after_ref[...] = jnp.zeros_like(code_after_ref)
+
+    @pl.when(has_upper)
+    def _():
+        for copy in to_upper:
+            copy.wait_send()
+        for copy in to_lower:
+            copy.wait_recv()
+
+    @pl.when(has_lower)
+    def _():
+        for copy in to_lower:
+            copy.wait_send()
+        for copy in to_upper:
+            copy.wait_recv()
+
+
+def exchange_kernel(
+    ranges,
+    ga_ref,
+    to_lower_ref,
+    to_upper_ref,
+    mine_ref,
+    theirs_ref,
+    sums_ref,
+    wpair_ref,
+    out_ref,
+    pair_out_ref,
+    total_ref,
+    from_lower,
+    from_upper,
+    got,
+    got_half,
+    part,
+    slots,
+    wpair_scr,
+    edge_sems,
+    core_sems,
+    scatter_sems,
+    gather_sems,
+):
+    me = lax.axis_index("atoms")
+    core = lax.axis_index("samples")
+    other = 1 - core
+    samples, atoms, channels = ga_ref.shape
+    span = to_lower_ref.shape[1]
+    chunk = part.shape[1]
+    half = ranges * chunk
+    has_lower, has_upper = me > 0, me < ranges - 1
+    lower, upper, peer = {"atoms": me - 1}, {"atoms": me + 1}, {"samples": other}
+    everyone = [{"atoms": lax.rem(me + d, ranges)} for d in range(1, ranges)]
+    barrier = pltpu.get_barrier_semaphore()
+    greet(barrier, [peer] + everyone)
+    pl.semaphore_wait(barrier, ranges)
+
+    half_copy = remote(
+        sums_ref.at[pl.ds(pl.multiple_of(other * half, 8), half)], got_half, core_sems, 0, peer
+    )
+    half_copy.start()
+    pair_copy = remote(theirs_ref, got, core_sems, 1, peer)
+    pair_copy.start()
+    up_copy = remote(to_upper_ref, from_lower, edge_sems, 0, upper)
+    down_copy = remote(to_lower_ref, from_upper, edge_sems, 1, lower)
+
+    half_copy.wait_recv()
+    own_half = pl.ds(pl.multiple_of(core * half, 8), half)
+    part[...] = (sums_ref[own_half, :] + got_half[...]).reshape(part.shape)
+    scatter = []
+    for d in range(1, ranges):
+        target = lax.rem(me + d, ranges)
+        copy = remote(part.at[target], slots.at[d - 1], scatter_sems, d - 1, everyone[d - 1])
+        copy.start()
+        scatter.append(copy)
+
+    @pl.when(has_upper)
+    def _():
+        up_copy.start()
+
+    @pl.when(has_lower)
+    def _():
+        down_copy.start()
+
+    pair_channels, heads = wpair_ref.shape
+    rows = mine_ref.shape[1] // heads
+    stack = heads * rows
+    lane = lax.broadcasted_iota(jnp.int32, (pair_channels, stack), 1)
+    values = wpair_ref[...].astype(F32)
+    wpair_rows = jnp.zeros((pair_channels, stack), F32)
+    for h in range(heads):
+        wpair_rows = jnp.where(lane // rows == h, values[:, h : h + 1], wpair_rows)
+    for i in range(rows):
+        wpair_scr[i * pair_channels : (i + 1) * pair_channels, :] = jnp.where(
+            lane % rows == i, wpair_rows, 0.0
+        ).astype(BF16)
+
+    for copy in scatter:
+        copy.wait_recv()
+    chunk_total = part[me]
+    for d in range(1, ranges):
+        chunk_total = chunk_total + slots[d - 1]
+    place = pl.ds(pl.multiple_of(core * half + me * chunk, 8), chunk)
+    total_ref[place, :] = chunk_total
+    gather = []
+    for d in range(1, ranges):
+        copy = remote(
+            total_ref.at[place], total_ref.at[place], gather_sems, d - 1, everyone[d - 1]
+        )
+        copy.start()
+        gather.append(copy)
+
+    pair_copy.wait_recv()
+
+    def one_window(w, carry):
+        both = mine_ref[w] + got[w].astype(F32)
+        high = both.astype(BF16)
+        low = (both - high.astype(F32)).astype(BF16)
+        weight = wpair_scr[...]
+        pair_out_ref[w] = (nn(weight, high) + nn(weight, low)).astype(BF16)
         return carry
 
-    lax.fori_loop(0, mine_ref.shape[0], one, 0)
+    lax.fori_loop(0, mine_ref.shape[0], one_window, 0)
+
+    for copy in gather:
+        copy.wait_recv()
+    last_copy = remote(
+        total_ref.at[own_half], total_ref.at[own_half], core_sems, 2, peer
+    )
+    last_copy.start()
+
+    @pl.when(has_lower)
+    def _():
+        down_copy.wait_send()
+        up_copy.wait_recv()
+
+    @pl.when(has_upper)
+    def _():
+        up_copy.wait_send()
+        down_copy.wait_recv()
+
+    @pl.when(jnp.logical_not(has_lower))
+    def _():
+        from_lower[...] = jnp.zeros_like(from_lower)
+
+    @pl.when(jnp.logical_not(has_upper))
+    def _():
+        from_upper[...] = jnp.zeros_like(from_upper)
+
+    def one_sample(s, carry):
+        out_ref[s, 0:span, :] = (ga_ref[s, 0:span, :] + from_lower[s].astype(F32)).astype(BF16)
+        out_ref[s, span : atoms - span, :] = ga_ref[s, span : atoms - span, :].astype(BF16)
+        out_ref[s, atoms - span : atoms, :] = (
+            ga_ref[s, atoms - span : atoms, :] + from_upper[s].astype(F32)
+        ).astype(BF16)
+        return carry
+
+    lax.fori_loop(0, samples, one_sample, 0)
+    half_copy.wait_send()
+    pair_copy.wait_send()
+    for copy in scatter + gather:
+        copy.wait_send()
+    last_copy.wait()
 
 
 def per_device(
@@ -239,44 +502,34 @@
     half = rows // 2
     ranges = lax.axis_size("atoms")
     wide = atoms + 2 * span
-    up = [(i, i + 1) for i in range(ranges - 1)]
-    down = [(i + 1, i) for i in range(ranges - 1)]
-
-    before = lax.ppermute(act[:, atoms - span :], "atoms", up)
-    after = lax.ppermute(act[:, :span], "atoms", down)
+    vmem = pl.BlockSpec(memory_space=pltpu.VMEM)
+    smem = pl.BlockSpec(memory_space=pltpu.SMEM)
     position = jnp.arange(atoms, dtype=jnp.int32)
     codes = jnp.where(position < atoms - padding[0], atom_token + 1, 0)
-    code_before = lax.ppermute(codes[atoms - span :], "atoms", up)
-    code_after = lax.ppermute(codes[:span], "atoms", down)
-    wide_codes = jnp.concatenate([code_before, codes, code_after]).astype(F32)
-    key_code = jnp.broadcast_to(wide_codes[:, None], (wide, stack))
-    query_code = jnp.tile((atom_token + 1).astype(F32).reshape(windows, 1, rows), (1, 1, heads))
-    anchor = lax.axis_index("atoms") * atoms
-    starts = (
-        jnp.clip(
-            anchor + rows * jnp.arange(windows, dtype=jnp.int32) + offsets,
-            0,
-            ranges * atoms - span,
-        )
-        - anchor
-        + span
-    )
-    me = lax.axis_index("samples").astype(jnp.int32)
-    eye = jnp.eye(rows, dtype=BF16)
-    wpair_big = (eye[:, None, None, :] * w_pair[None, :, :, None]).reshape(
-        rows * pair_channels, stack
-    )
-    eye_half = jnp.eye(half, dtype=BF16)
-    wpair_half = (eye_half[:, None, None, :] * w_pair[None, :, :, None]).reshape(
-        half * pair_channels, heads * half
-    )
-    wtoken_row = jnp.repeat(w_token, rows)[None, :]
-    weights = jnp.stack([w_query, w_key, w_value, w_gate, w_out])
+    codes = codes.reshape(atoms // span, 1, span)
+    query_code = jnp.tile((atom_token + 1).reshape(windows, 1, rows), (1, 1, heads))
+
+    def first_kernel(*refs):
+        halo_kernel(ranges, span, *refs)
+
+    before, after, code_before, code_after = pl.pallas_call(
+        first_kernel,
+        out_shape=(
+            jax.ShapeDtypeStruct((samples, span, channels), BF16),
+            jax.ShapeDtypeStruct((samples, span, channels), BF16),
+            jax.ShapeDtypeStruct((1, 1, span), jnp.int32),
+            jax.ShapeDtypeStruct((1, 1, span), jnp.int32),
+        ),
+        in_specs=[pl.BlockSpec(memory_space=pl.ANY), vmem],
+        out_specs=(vmem,) * 4,
+        scratch_shapes=[pltpu.SemaphoreType.DMA((2, 4))],
+        compiler_params=pltpu.CompilerParams(collective_id=0, has_side_effects=True),
+        name="halo",
+    )(act, codes)
 
     together = 4 if samples % 4 == 0 else 1
-    vmem = pl.BlockSpec(memory_space=pltpu.VMEM)
-    smem = pl.BlockSpec(memory_space=pltpu.SMEM)
-    sum_rows = 5 * channels + pair_channels + 8
+    chunk = 8 * pl.cdiv(5 * channels + pair_channels + 1, 16 * ranges)
+    sum_rows = 2 * ranges * chunk
 
     def kernel(*refs):
         attention_kernel(heads, together, *refs)
@@ -291,7 +544,7 @@
             jax.ShapeDtypeStruct((windows, heads * half, span), BF16),
             jax.ShapeDtypeStruct((sum_rows, channels), F32),
         ),
-        in_specs=[smem, smem] + [vmem] * 10,
+        in_specs=[smem, smem] + [vmem] * 15,
         out_specs=(vmem,) * 6,
         scratch_shapes=[
             pltpu.VMEM((samples, wide, channels), BF16),
@@ -309,45 +562,62 @@
             pltpu.VMEM((span, stack), F32),
             pltpu.VMEM((span, stack), F32),
             pltpu.VMEM((span, stack), F32),
+            pltpu.VMEM((wide, stack), F32),
+            pltpu.VMEM((rows * pair_channels, stack), BF16),
         ],
         compiler_params=pltpu.CompilerParams(vmem_limit_bytes=56 * 1024 * 1024),
         name="attention",
     )(
-        starts,
-        me.reshape(1),
+        offsets,
+        w_token,
         act,
         before,
         after,
         grad_out,
         pair.reshape(windows, rows * pair_channels, span),
-        weights,
-        wpair_big,
-        wtoken_row,
-        key_code,
+        w_query,
+        w_key,
+        w_value,
+        w_gate,
+        w_out,
+        w_pair,
+        codes,
+        code_before,
+        code_after,
         query_code,
     )
 
-    from_upper = lax.ppermute(to_lower, "atoms", down).astype(F32)
-    from_lower = lax.ppermute(to_upper, "atoms", up).astype(F32)
-    count = lax.axis_size("samples")
-    got = lax.ppermute(theirs, "samples", [(i, (i + 1) % count) for i in range(count)])
-    total = lax.psum(sums, ("atoms", "samples"))
-
-    grad_act = jnp.concatenate(
-        [
-            ga[:, :span] + from_lower,
-            ga[:, span : atoms - span],
-            ga[:, atoms - span :] + from_upper,
+    def last_kernel(*refs):
+        exchange_kernel(ranges, *refs)
+
+    edge = pltpu.VMEM((samples, span, channels), BF16)
+    grad_act, grad_pair, total = pl.pallas_call(
+        last_kernel,
+        out_shape=(
+            jax.ShapeDtypeStruct((samples, atoms, channels), BF16),
+            jax.ShapeDtypeStruct((windows, half * pair_channels, span), BF16),
+            jax.ShapeDtypeStruct((sum_rows, channels), F32),
+        ),
+        in_specs=[vmem] * 7,
+        out_specs=(vmem,) * 3,
+        scratch_shapes=[
+            edge,
+            edge,
+            pltpu.VMEM((windows, heads * half, span), BF16),
+            pltpu.VMEM((ranges * chunk, channels), F32),
+            pltpu.VMEM((ranges, chunk, channels), F32),
+            pltpu.VMEM((ranges - 1, chunk, channels), F32),
+            pltpu.VMEM((half * pair_channels, heads * half), BF16),
+            pltpu.SemaphoreType.DMA((2, 2)),
+            pltpu.SemaphoreType.DMA((2, 3)),
+            pltpu.SemaphoreType.DMA((2, ranges - 1)),
+            pltpu.SemaphoreType.DMA((2, ranges - 1)),
         ],
-        axis=1,
-    ).astype(BF16)
-    grad_pair = pl.pallas_call(
-        pair_kernel,
-        out_shape=jax.ShapeDtypeStruct((windows, half * pair_channels, span), BF16),
-        in_specs=[vmem] * 3,
-        out_specs=vmem,
-        name="pair_grad",
-    )(mine, got, wpair_half).reshape(windows, half, pair_channels, span)
+        compiler_params=pltpu.CompilerParams(
+            collective_id=1, has_side_effects=True, vmem_limit_bytes=40 * 1024 * 1024
+        ),
+        name="exchange",
+    )(ga, to_lower, to_upper, mine, theirs, sums, w_pair)
 
     base = 5 * channels
     grad_weights = total[:base].reshape(5, channels, channels)
@@ -355,6 +625,7 @@
         total[base : base + pair_channels].reshape(pair_channels, heads, rows), axis=-1
     )
     grad_token_weight = jnp.sum(total[base + pair_channels].reshape(heads, rows), axis=-1)
+    grad_pair = grad_pair.reshape(windows, half, pair_channels, span)
     return (grad_act, grad_pair, grad_weights, grad_pair_weight, grad_token_weight)
 
 

time: 206 us -> 109 us (0.53)
  waiting for transfers between devices: 90.8 us -> 0 us
  Pallas kernels: 59.7 us -> 92.5 us
  starting transfers between devices: 20.4 us -> 0 us
  between operations: 14.9 us -> 1.33 us
  other arithmetic: 4.81 us -> 1.41 us
    psum x1 -> x0, waiting for transfers between devices: 88.1 us -> none  [per_device(): total = lax.psum(sums, ('atoms', 'samples'))]
    pallas_call x1 -> x2, Pallas kernels: 5.74 us -> 38.2 us  [the longest x1 21.8 us: per_device(): pl.pallas_call(last_kernel, out_shape=(jax.ShapeDtypeStruct((samples, ato...]
    ppermute x7 -> x0, starting transfers between devices: 20.4 us -> none  [the longest x1 4.82 us: per_device(): from_upper = lax.ppermute(to_lower, 'atoms', down).astype(F32)]
    unnamed x26 -> x18, local copies, waits for them, and re-layouts: 4.48 us -> 10.8 us
    ppermute x7 -> x0, waiting for transfers between devices: 2.71 us -> none  [the longest x1 2.7 us: per_device(): after = lax.ppermute(act[:, :span], 'atoms', down)]
    slice x3 -> x0, local copies, waits for them, and re-layouts: 2.61 us -> none  [the longest x1 1.53 us: per_device(): ga[:, span:atoms - span]]
  transfers between devices with their start and end apart: 8 -> 0, of which waited for: 2 -> 0; matrix products, arithmetic and copies ran while one was open for 8% -> 0% of each run, Pallas kernels for 0% -> 0%
where the time goes in v2:
time: 109 us; the launch traced here: 108 us
  Pallas kernels  92.5 us (85%)
  local copies, waits for them, and re-layouts  13.1 us (12%)
  other arithmetic  1.41 us (1%)
  between operations  1.33 us (1%)
    pallas_call x1, Pallas kernels, per_device(): pl.pallas_call(kernel, out_shape=(jax.ShapeDtypeStruct((samples, atoms, c...  54.2 us
    pallas_call x1, Pallas kernels, per_device(): pl.pallas_call(last_kernel, out_shape=(jax.ShapeDtypeStruct((samples, ato...  21.8 us
    pallas_call x1, Pallas kernels, per_device(): pl.pallas_call(first_kernel, out_shape=(jax.ShapeDtypeStruct((samples, sp...  16.4 us
    unnamed x18, local copies, waits for them, and re-layouts  10.8 us

profile of v2, /device:TPU:8, one launch (start us, length us, event | category | flops | bytes accessed | tf_op | source)
XLA Modules:
  0.0 108.3 jit_solution(10358215895295088368)
XLA Ops:
  1.3 1.4 %copy.20.refs_12_.refs_6_ = bf16[16,4]{1,0:T(8,128)(2,1)} copy(bf16[16,4]{0,1:T(4,128)(2,1)} %param.21) | data formatting | bytes 256 | tf_op args[8]
  2.6 0.7 broadcast_add_fusion
  3.3 0.6 reshape.33.refs_1_.refs_13_
  3.9 0.1 tile.10
  4.0 0.7 tile.12.refs_16_
  4.7 16.4 %halo.1 = (bf16[8,128,128]{2,1,0:T(8,128)(2,1)}, bf16[8,128,128]{2,1,0:T(8,128)(2,1)}, s32[1,1,128]{2,1,0:T(1,128)}, s32[1,1,128]{2,1,0:T(1,128)}) custom-call(bf16[8,640,128]{2,1,0:T(8,128)(2,1)} %refs_2_.1, s32[5,1,128]{2,1,0:T(1,128)} %reshape.33.refs_1_.refs_13_), custom_call_target="tpu_custom_call" | custom-call | tf_op jit(solution)/shard_map/halo/pallas_call | solution.py:515
  21.1 0.0 copy-start.6
  21.1 54.2 %attention.1 = (f32[8,640,128]{2,1,0:T(8,128)}, bf16[8,128,128]{2,1,0:T(8,128)(2,1)}, bf16[8,128,128]{2,1,0:T(8,128)(2,1)}, f32[20,64,128]{2,1,0:T(8,128)}, bf16...) custom-call(s32[20]{0:T(128)} %refs_0_.3, f32[4]{0:T(128)} %refs_1_.1, bf16[8,640,128]{2,1,0:T(8,128)(2,1)} %refs_2_.1, ...), custom_call_target="tpu_custom_call" | custom-call | tf_op jit(solution)/shard_map/attention/pallas_call | solution.py:537
  75.4 0.0 copy-done.6
  75.4 0.0 copy-start
  75.4 1.7 %copy-done = f32[8,640,128]{2,1,0:T(8,128)S(1)} copy-done((f32[8,640,128]{2,1,0:T(8,128)S(1)}, f32[8,640,128]{2,1,0:T(8,128)}, u32[]{:S(2)}) %copy-start) | copy-done | bytes 2621464
  77.1 0.0 copy-start.1
  77.1 1.1 %copy-done.1 = f32[20,64,128]{2,1,0:T(8,128)S(1)} copy-done((f32[20,64,128]{2,1,0:T(8,128)S(1)}, f32[20,64,128]{2,1,0:T(8,128)}, u32[]{:S(2)}) %copy-start.1) | copy-done | bytes 655384
  78.2 0.0 copy-start.2
  78.2 1.0 copy-done.2
  79.2 0.0 copy-start.3
  79.2 1.0 copy-done.3
  80.2 0.0 copy-start.4
  80.2 0.9 copy-done.4
  81.1 0.0 copy-start.5
  81.1 0.9 copy-done.5
  82.1 21.8 %exchange.1 = (bf16[8,640,128]{2,1,0:T(8,128)(2,1)S(1)}, bf16[20,256,128]{2,1,0:T(8,128)(2,1)S(1)}, f32[768,128]{1,0:T(8,128)S(1)}) custom-call(f32[8,640,128]{2,1,0:T(8,128)S(1)} %copy-done, bf16[8,128,128]{2,1,0:T(8,128)(2,1)S(1)} %copy-done.4, bf16[8,128,128]{2,1,0:T(8,128)(2,1)S(1)} %copy-done.5, f32[20,64,128]{2,1,0:T(8,128)S(1)} %copy-done.1, ...), custom_call_target="tpu_custom_call" | custom-call | tf_op jit(solution)/shard_map/exchange/pallas_call | solution.py:594
  103.9 0.1 reshape_squeeze.3
  104.0 0.6 reduce_sum.19
  104.6 0.7 slice.9
  105.4 0.1 reshape.37
  105.5 0.1 reduce_sum.18
  105.6 0.7 copy.22
  106.2 1.1 copy.26
  107.3 1.1 copy.27
  (3 shorter events, 0.0 us)
Async XLA Ops:
  21.1 54.2 %copy-start.6 = (bf16[16,4]{1,0:T(8,128)(2,1)S(1)}, bf16[16,4]{1,0:T(8,128)(2,1)}, u32[]{:S(2)}) copy-start(bf16[16,4]{1,0:T(8,128)(2,1)} %copy.20.refs_12_.refs_6_) | copy-start | bytes 388
  75.4 1.7 %copy-start = (f32[8,640,128]{2,1,0:T(8,128)S(1)}, f32[8,640,128]{2,1,0:T(8,128)}, u32[]{:S(2)}) copy-start(f32[8,640,128]{2,1,0:T(8,128)} %get-tuple-element.22.refs_0_) | copy-start | bytes 7864324
  77.1 1.1 %copy-start.1 = (f32[20,64,128]{2,1,0:T(8,128)S(1)}, f32[20,64,128]{2,1,0:T(8,128)}, u32[]{:S(2)}) copy-start(f32[20,64,128]{2,1,0:T(8,128)} %get-tuple-element.25.refs_3_) | copy-start | bytes 1966084
  78.2 1.0 copy-start.2
  79.2 1.0 copy-start.3
  80.2 0.9 copy-start.4
  81.1 0.9 copy-start.5

commit v3 on v2

--- a/solution.py
+++ b/solution.py
@@ -379,6 +379,14 @@
     up_copy = remote(to_upper_ref, from_lower, edge_sems, 0, upper)
     down_copy = remote(to_lower_ref, from_upper, edge_sems, 1, lower)
 
+    @pl.when(has_upper)
+    def _():
+        up_copy.start()
+
+    @pl.when(has_lower)
+    def _():
+        down_copy.start()
+
     half_copy.wait_recv()
     own_half = pl.ds(pl.multiple_of(core * half, 8), half)
     part[...] = (sums_ref[own_half, :] + got_half[...]).reshape(part.shape)
@@ -388,14 +396,6 @@
         copy = remote(part.at[target], slots.at[d - 1], scatter_sems, d - 1, everyone[d - 1])
         copy.start()
         scatter.append(copy)
-
-    @pl.when(has_upper)
-    def _():
-        up_copy.start()
-
-    @pl.when(has_lower)
-    def _():
-        down_copy.start()
 
     pair_channels, heads = wpair_ref.shape
     rows = mine_ref.shape[1] // heads
@@ -504,6 +504,7 @@
     wide = atoms + 2 * span
     vmem = pl.BlockSpec(memory_space=pltpu.VMEM)
     smem = pl.BlockSpec(memory_space=pltpu.SMEM)
+    anywhere = pl.BlockSpec(memory_space=pl.ANY)
     position = jnp.arange(atoms, dtype=jnp.int32)
     codes = jnp.where(position < atoms - padding[0], atom_token + 1, 0)
     codes = codes.reshape(atoms // span, 1, span)
@@ -527,7 +528,7 @@
         name="halo",
     )(act, codes)
 
-    together = 4 if samples % 4 == 0 else 1
+    together = 8 if samples % 8 == 0 else 1
     chunk = 8 * pl.cdiv(5 * channels + pair_channels + 1, 16 * ranges)
     sum_rows = 2 * ranges * chunk
 
@@ -598,7 +599,7 @@
             jax.ShapeDtypeStruct((windows, half * pair_channels, span), BF16),
             jax.ShapeDtypeStruct((sum_rows, channels), F32),
         ),
-        in_specs=[vmem] * 7,
+        in_specs=[vmem, anywhere, anywhere, vmem, anywhere, vmem, vmem],
         out_specs=(vmem,) * 3,
         scratch_shapes=[
             edge,

time: 109 us -> 94.4 us (0.87)
  Pallas kernels: 92.5 us -> 76.8 us
    pallas_call x1, Pallas kernels: 54.2 us -> 37.3 us  [per_device(): pl.pallas_call(kernel, out_shape=(jax.ShapeDtypeStruct((samples, atoms, c...]
    pallas_call x1, Pallas kernels: 21.8 us -> 23.1 us  [per_device(): pl.pallas_call(last_kernel, out_shape=(jax.ShapeDtypeStruct((samples, ato...]
where the time goes in v3:
time: 94.4 us; the launch traced here: 92.6 us
  Pallas kernels  76.8 us (81%)
  local copies, waits for them, and re-layouts  13.1 us (14%)
  other arithmetic  1.41 us (1%)
  between operations  1.33 us (1%)
    pallas_call x1, Pallas kernels, per_device(): pl.pallas_call(kernel, out_shape=(jax.ShapeDtypeStruct((samples, atoms, c...  37.3 us
    pallas_call x1, Pallas kernels, per_device(): pl.pallas_call(last_kernel, out_shape=(jax.ShapeDtypeStruct((samples, ato...  23.1 us
    pallas_call x1, Pallas kernels, per_device(): pl.pallas_call(first_kernel, out_shape=(jax.ShapeDtypeStruct((samples, sp...  16.4 us
    unnamed x18, local copies, waits for them, and re-layouts  10.8 us

profile of v3, /device:TPU:8, one launch (start us, length us, event | category | flops | bytes accessed | tf_op | source)
XLA Modules:
  0.0 92.6 jit_solution(17616847454511306716)
XLA Ops:
  1.3 1.4 %copy.20.refs_12_.refs_6_ = bf16[16,4]{1,0:T(8,128)(2,1)} copy(bf16[16,4]{0,1:T(4,128)(2,1)} %param.21) | data formatting | bytes 256 | tf_op args[8]
  2.6 0.7 broadcast_add_fusion
  3.3 0.6 reshape.33.refs_1_.refs_13_
  3.9 0.1 tile.10
  4.0 0.7 tile.12.refs_16_
  4.7 16.4 %halo.1 = (bf16[8,128,128]{2,1,0:T(8,128)(2,1)}, bf16[8,128,128]{2,1,0:T(8,128)(2,1)}, s32[1,1,128]{2,1,0:T(1,128)}, s32[1,1,128]{2,1,0:T(1,128)}) custom-call(bf16[8,640,128]{2,1,0:T(8,128)(2,1)} %refs_2_.1, s32[5,1,128]{2,1,0:T(1,128)} %reshape.33.refs_1_.refs_13_), custom_call_target="tpu_custom_call" | custom-call | tf_op jit(solution)/shard_map/halo/pallas_call | solution.py:516
  21.1 0.0 copy-start.6
  21.1 37.3 %attention.1 = (f32[8,640,128]{2,1,0:T(8,128)}, bf16[8,128,128]{2,1,0:T(8,128)(2,1)}, bf16[8,128,128]{2,1,0:T(8,128)(2,1)}, f32[20,64,128]{2,1,0:T(8,128)}, bf16...) custom-call(s32[20]{0:T(128)} %refs_0_.3, f32[4]{0:T(128)} %refs_1_.1, bf16[8,640,128]{2,1,0:T(8,128)(2,1)} %refs_2_.1, ...), custom_call_target="tpu_custom_call" | custom-call | tf_op jit(solution)/shard_map/attention/pallas_call | solution.py:538
  58.4 0.0 copy-done.6
  58.4 0.0 copy-start
  58.4 1.7 %copy-done = f32[8,640,128]{2,1,0:T(8,128)S(1)} copy-done((f32[8,640,128]{2,1,0:T(8,128)S(1)}, f32[8,640,128]{2,1,0:T(8,128)}, u32[]{:S(2)}) %copy-start) | copy-done | bytes 2621464
  60.2 0.0 copy-start.1
  60.2 1.1 %copy-done.1 = f32[20,64,128]{2,1,0:T(8,128)S(1)} copy-done((f32[20,64,128]{2,1,0:T(8,128)S(1)}, f32[20,64,128]{2,1,0:T(8,128)}, u32[]{:S(2)}) %copy-start.1) | copy-done | bytes 655384
  61.3 0.0 copy-start.2
  61.3 1.0 %copy-done.2 = f32[768,128]{1,0:T(8,128)S(1)} copy-done((f32[768,128]{1,0:T(8,128)S(1)}, f32[768,128]{1,0:T(8,128)}, u32[]{:S(2)}) %copy-start.2) | copy-done | bytes 393240
  62.3 0.0 copy-start.3
  62.3 1.0 %copy-done.3 = bf16[20,64,128]{2,1,0:T(8,128)(2,1)S(1)} copy-done((bf16[20,64,128]{2,1,0:T(8,128)(2,1)S(1)}, bf16[20,64,128]{2,1,0:T(8,128)(2,1)}, u32[]{:S(2)}) %copy-start.3) | copy-done | bytes 327704
  63.2 0.0 copy-start.4
  63.2 0.9 %copy-done.4 = bf16[8,128,128]{2,1,0:T(8,128)(2,1)S(1)} copy-done((bf16[8,128,128]{2,1,0:T(8,128)(2,1)S(1)}, bf16[8,128,128]{2,1,0:T(8,128)(2,1)}, u32[]{:S(2)}) %copy-start.4) | copy-done | bytes 262168
  64.2 0.0 copy-start.5
  64.2 0.9 %copy-done.5 = bf16[8,128,128]{2,1,0:T(8,128)(2,1)S(1)} copy-done((bf16[8,128,128]{2,1,0:T(8,128)(2,1)S(1)}, bf16[8,128,128]{2,1,0:T(8,128)(2,1)}, u32[]{:S(2)}) %copy-start.5) | copy-done | bytes 262168
  65.1 23.1 %exchange.1 = (bf16[8,640,128]{2,1,0:T(8,128)(2,1)S(1)}, bf16[20,256,128]{2,1,0:T(8,128)(2,1)S(1)}, f32[768,128]{1,0:T(8,128)S(1)}) custom-call(f32[8,640,128]{2,1,0:T(8,128)S(1)} %copy-done, bf16[8,128,128]{2,1,0:T(8,128)(2,1)S(1)} %copy-done.4, bf16[8,128,128]{2,1,0:T(8,128)(2,1)S(1)} %copy-done.5, f32[20,64,128]{2,1,0:T(8,128)S(1)} %copy-done.1, ...), custom_call_target="tpu_custom_call" | custom-call | tf_op jit(solution)/shard_map/exchange/pallas_call | solution.py:595
  88.2 0.1 reshape_squeeze.3
  88.3 0.6 reduce_sum.19
  89.0 0.7 slice.9
  89.7 0.1 reshape.37
  89.8 0.1 reduce_sum.18
  89.9 0.7 copy.22
  90.5 1.1 %copy.26 = bf16[8,640,128]{2,1,0:T(8,128)(2,1)} copy(bf16[8,640,128]{2,1,0:T(8,128)(2,1)S(1)} %get-tuple-element.43) | data formatting | bytes 2621440
  91.6 1.1 %copy.27 = bf16[20,16,16,128]{3,2,1,0:T(8,128)(2,1)} copy(bf16[20,16,16,128]{3,2,1,0:T(8,128)(2,1)S(1)} %bitcast.4) | data formatting | bytes 2621440
  (3 shorter events, 0.0 us)
Async XLA Ops:
  21.1 37.3 %copy-start.6 = (bf16[16,4]{1,0:T(8,128)(2,1)S(1)}, bf16[16,4]{1,0:T(8,128)(2,1)}, u32[]{:S(2)}) copy-start(bf16[16,4]{1,0:T(8,128)(2,1)} %copy.20.refs_12_.refs_6_) | copy-start | bytes 388
  58.4 1.7 %copy-start = (f32[8,640,128]{2,1,0:T(8,128)S(1)}, f32[8,640,128]{2,1,0:T(8,128)}, u32[]{:S(2)}) copy-start(f32[8,640,128]{2,1,0:T(8,128)} %get-tuple-element.22.refs_0_) | copy-start | bytes 7864324
  60.2 1.1 %copy-start.1 = (f32[20,64,128]{2,1,0:T(8,128)S(1)}, f32[20,64,128]{2,1,0:T(8,128)}, u32[]{:S(2)}) copy-start(f32[20,64,128]{2,1,0:T(8,128)} %get-tuple-element.25.refs_3_) | copy-start | bytes 1966084
  61.3 1.0 %copy-start.2 = (f32[768,128]{1,0:T(8,128)S(1)}, f32[768,128]{1,0:T(8,128)}, u32[]{:S(2)}) copy-start(f32[768,128]{1,0:T(8,128)} %get-tuple-element.27.refs_5_) | copy-start | bytes 1179652
  62.3 1.0 %copy-start.3 = (bf16[20,64,128]{2,1,0:T(8,128)(2,1)S(1)}, bf16[20,64,128]{2,1,0:T(8,128)(2,1)}, u32[]{:S(2)}) copy-start(bf16[20,64,128]{2,1,0:T(8,128)(2,1)} %get-tuple-element.26.refs_4_) | copy-start | bytes 983044
  63.2 0.9 %copy-start.4 = (bf16[8,128,128]{2,1,0:T(8,128)(2,1)S(1)}, bf16[8,128,128]{2,1,0:T(8,128)(2,1)}, u32[]{:S(2)}) copy-start(bf16[8,128,128]{2,1,0:T(8,128)(2,1)} %get-tuple-element.23.refs_1_) | copy-start | bytes 786436
  64.2 0.9 %copy-start.5 = (bf16[8,128,128]{2,1,0:T(8,128)(2,1)S(1)}, bf16[8,128,128]{2,1,0:T(8,128)(2,1)}, u32[]{:S(2)}) copy-start(bf16[8,128,128]{2,1,0:T(8,128)(2,1)} %get-tuple-element.24.refs_2_) | copy-start | bytes 786436
